TPU v7x, 32 devices: a whole 2x2x4 slice. The times are simulated.
32 devices in a mesh: section: 4 (over x, core), fsdp: 8 (over z, y).
Axes of the slice: x: 2, y: 2, z: 4, core: 2. Of those that a mesh axis runs over, the one named last changes fastest.
Arguments:
- produced: bfloat16 [4, 24, 256, 4096], P('section', 'fsdp'), may hold values from -6 to 6
- lengths: int32 [4, 24], P('section', 'fsdp'), may hold values from 64 to 256, as said below
- active: int32 [4, 24, 4], P('section', 'fsdp'), may hold values from 0 to 7, all different within a row
- window_blocks: int32 [8], replicated, may hold values from 0 to 249, as said below
- triplets: int32 [4, 8, 3], P('section'), may hold values from 0 to 23, as said below
- teacher: float32 [4, 8], P('section'), may hold values from -60 to 60
- norm_gain: bfloat16 [4096], P('fsdp'), may hold values from 0.5 to 1.5
- head: bfloat16 [32000, 4096], P(None, 'fsdp'), may hold values from -0.09375 to 0.09375
Outputs:
- losses: float32 [4], P('section')
- produced_grad: bfloat16 [4, 24, 256, 4096], P('section', 'fsdp')
- head_grad: float32 [1024, 4096], P(None, 'fsdp')
- gain_grad: float32 [4096], P('fsdp')
Inputs may be any that keep to these rules, and one draw needn't show every extreme that they name: `lengths`: every device's first sequence holds 256 tokens, and some sequence holds 64. `active`: each row names 4 different slots. `window_blocks`: ids are distinct. `triplets`: each sequence of a group stands in exactly one triplet, once.
All inputs are finite; a program needn't handle non-finite values.
Results may differ from a plain program's by a relative error of at most 0.0051.
Values may be sent and summed in bfloat16 or wider, within the bound.
A program may use at most 192 MiB of HBM per device.

v0:
```python
import jax
import jax.numpy as jnp
from jax import lax
from jax.sharding import PartitionSpec as P

D = 4096
BLOCK = 128
U = 8
LEN = 256
SEQ_DEV = 3


eps = 1e-05
loss_scale = 256.0


def passed_along(block, axis, distance):
    devices = range(lax.axis_size(axis))
    route = [((i - distance) % len(devices), i) for i in devices]
    return lax.ppermute(block, axis, route)


def pool_terms(logits):
    smooth = jax.nn.softplus(logits)
    return (jnp.log1p(smooth), jax.nn.sigmoid(logits) / (1.0 + smooth))


def local(produced, lengths, active, window_blocks, triplets, teacher, norm_gain, head):
    hidden, seq_lengths, block_slots = passed_along((produced, lengths, active), "section", 1)
    columns = head.shape[1]
    local_rows = head.reshape(head.shape[0] // BLOCK, BLOCK, columns)[window_blocks].reshape(
        U * BLOCK, columns
    )
    window, gain_full = (
        lax.all_gather(local_rows, "fsdp", axis=1, tiled=True),
        lax.all_gather(norm_gain, "fsdp", axis=0, tiled=True),
    )
    gain32 = gain_full.astype(jnp.float32)
    tokens = hidden.reshape(SEQ_DEV * LEN, D)
    widened = tokens.astype(jnp.float32)
    inv_rms = lax.rsqrt(jnp.mean(widened * widened, axis=1, keepdims=True) + eps)
    normed = (widened * inv_rms * gain32).astype(jnp.bfloat16)
    seq_len_row = seq_lengths[0]
    slot_table = block_slots[0]
    position = jnp.arange(LEN, dtype=jnp.int32)
    weight = (position[None, :] < seq_len_row[:, None]).astype(jnp.float32) / seq_len_row[
        :, None
    ].astype(jnp.float32)
    slot_range = jnp.arange(U, dtype=jnp.int32)
    onehot = (slot_table[:, :, None] == slot_range[None, None, :]).astype(jnp.float32)
    chosen = jnp.sum(onehot, axis=1)
    spread = jnp.repeat(chosen, BLOCK, axis=1)
    logits = jnp.einsum("td,jd->tj", normed, window, preferred_element_type=jnp.float32)
    values, slopes = pool_terms(logits.reshape(SEQ_DEV, LEN, U * BLOCK))
    pooled = jnp.sum(weight[:, :, None] * values, axis=1) * spread
    all_pooled = lax.all_gather(pooled, "fsdp", axis=0, tiled=True)
    triplet_rows = triplets[0]
    query_rows = all_pooled[triplet_rows[:, 0]]
    positive = all_pooled[triplet_rows[:, 1]]
    negative = all_pooled[triplet_rows[:, 2]]
    margin = jnp.sum(query_rows * (positive - negative), axis=1)
    deviation = margin - teacher[0]
    loss_value = jnp.mean(deviation * deviation)
    grad_margin = loss_scale * 2.0 * deviation / triplets.shape[1]
    first_row = lax.axis_index("fsdp") * SEQ_DEV
    own_rows = first_row + jnp.arange(SEQ_DEV, dtype=jnp.int32)
    query_hits = (triplet_rows[:, 0][:, None] == own_rows[None, :]).astype(jnp.float32)
    positive_hits = (triplet_rows[:, 1][:, None] == own_rows[None, :]).astype(jnp.float32)
    negative_hits = (triplet_rows[:, 2][:, None] == own_rows[None, :]).astype(jnp.float32)
    query_term = grad_margin[:, None] * (positive - negative)
    other_term = grad_margin[:, None] * query_rows
    grad_pooled = jnp.einsum("ts,tj->sj", query_hits, query_term, precision=lax.Precision.HIGHEST)
    grad_pooled = grad_pooled + jnp.einsum(
        "ts,tj->sj", positive_hits, other_term, precision=lax.Precision.HIGHEST
    )
    grad_pooled = grad_pooled - jnp.einsum(
        "ts,tj->sj", negative_hits, other_term, precision=lax.Precision.HIGHEST
    )
    grad_values = grad_pooled * spread
    grad_logits = (weight[:, :, None] * grad_values[:, None, :] * slopes).astype(jnp.bfloat16)
    grad_logits = grad_logits.reshape(SEQ_DEV * LEN, U * BLOCK)
    grad_normed = jnp.dot(grad_logits, window, preferred_element_type=jnp.float32)
    head_part = jnp.einsum("tj,td->jd", grad_logits, normed, preferred_element_type=jnp.float32)
    gain_part = jnp.sum(grad_normed * widened * inv_rms, axis=0)
    scaled = grad_normed * gain32
    grad_tokens = inv_rms * scaled - widened * (inv_rms * inv_rms * inv_rms) * jnp.mean(
        scaled * widened, axis=1, keepdims=True
    )
    outgoing = grad_tokens.astype(jnp.bfloat16).reshape(1, SEQ_DEV, LEN, D)
    sent_back = passed_along(outgoing, "section", -1)
    head_piece, gain_piece = (
        lax.psum_scatter(head_part, "fsdp", scatter_dimension=1, tiled=True),
        lax.psum_scatter(gain_part, "fsdp", scatter_dimension=0, tiled=True),
    )
    head_piece, gain_piece = lax.psum((head_piece, gain_piece), "section")
    return (loss_value.reshape(1), sent_back, head_piece, gain_piece)


def solution(mesh):
    return jax.shard_map(
        local,
        mesh=mesh,
        in_specs=(
            P("section", "fsdp", None, None),
            P("section", "fsdp"),
            P("section", "fsdp", None),
            P(),
            P("section", None, None),
            P("section", None),
            P("fsdp"),
            P(None, "fsdp"),
        ),
        out_specs=(P("section"), P("section", "fsdp", None, None), P(None, "fsdp"), P("fsdp")),
        check_vma=False,
    )
```

profile of v0, /device:TPU:0, one launch (start us, length us, event | category | flops | bytes accessed | tf_op | source)
XLA Modules:
  0.0 551.3 jit_solution(239315944673984651)
XLA Ops:
  7.2 0.0 all-gather.4.cloned.1.call-start
  7.2 0.7 compare_select_fusion.3
  7.9 2.9 gather_fusion
  10.7 0.0 all-gather.4.cloned.1.call-update
  10.8 0.0 reduce-scatter.2.cloned.1.call-start
  10.8 0.5 collective-permute-start.1
  11.4 2.6 collective-permute-start
  13.9 0.1 collective-permute-start.2
  14.0 0.7 copy.21
  14.7 0.7 reshape.188
  15.4 26.9 %all-gather = bf16[8,1,512]{2,1,0:T(2,128)(2,1)S(1)} all-gather(bf16[1,1,512]{2,1,0:T(2,128)(2,1)S(1)} %reshape.188), channel_id=1, replica_groups=mesh['section'=4,'fsdp'=8] {'fsdp'}, dimensions={0}, use_global_device_ids=true | all-gather | bytes 9216 | tf_op jit(solution)/shard_map/all_gather | solution.py:36
  42.3 39.9 %collective-permute-done = s32[1,3]{1,0:T(1,128)S(1)} collective-permute-done((s32[1,3]{1,0:T(1,128)}, s32[1,3]{1,0:T(1,128)S(1)}, u32[]{:S(2)}, u32[]{:S(2)}) %collective-permute-start) | collective-permute-done | bytes 44 | tf_op jit(solution)/shard_map/ppermute | solution.py:20
  82.3 0.1 convert_divide_fusion
  82.3 0.0 collective-permute-done.2
  82.3 0.1 convert_reduce_fusion
  82.4 0.1 broadcast_bitcast_fusion
  82.5 4.1 fusion.3
  86.7 8.2 %fusion.5 = bf16[1,3,256,4096]{3,2,1,0:T(8,128)(2,1)} fusion(bf16[1,3,256,4096]{3,2,1,0:T(8,128)(2,1)} %collective-permute-done.1, f32[4096]{0:T(1024)S(1)} %bitcast.83, f32[3,256]{1,0:T(4,128)S(1)} %add_rsqrt_fusion), kind=kLoop, calls=%fused_computation.15 | loop fusion | flops 12582912 | bytes 12602368 | tf_op jit(solution)/shard_map/convert_element_type | solution.py:42
  94.9 43.9 %all-gather.4.cloned.1.call-done = bf16[1024,4096]{1,0:T(8,128)(2,1)} async-done(((bf16[1024,512]{1,0:T(8,128)(2,1)}), bf16[1024,4096]{1,0:T(8,128)(2,1)}) %all-gather.4.cloned.1.call-update) | async-done | bytes 8388624 | tf_op jit(solution)/shard_map/all_gather | solution.py:35
  138.8 11.2 %fusion.18 = (u8[256,1024]{1,0:T(8,128)(4,1)S(1)}, f32[3,256,1024]{2,1,0:T(8,128)S(1)}) fusion(bf16[1024,4096]{1,0:T(8,128)(2,1)} %all-gather.4.cloned.1.call-done, bf16[1,3,256,4096]{3,2,1,0:T(8,128)(2,1)} %collective-permute-done.1, f32[4096]{0:T(1024)S(1)} %bitcast.84, f32[3,256]{1,0:T(4,128)S(1)} %add_rsqrt_fusion), kind=kOutput, calls=%fused_computation.34 | convolution fusion | flops 6458703872 | bytes 18107392 | tf_op jit(solution)/shard_map/td,jd->tj/dot_general | solution.py:53
  150.0 3.0 multiply_reduce_fusion
  153.0 30.7 %all-gather.1 = f32[8,3,1024]{2,1,0:T(4,128)S(1)} all-gather(f32[1,3,1024]{2,1,0:T(4,128)S(1)} %fusion.23), channel_id=1, replica_groups=mesh['section'=4,'fsdp'=8] {'fsdp'}, dimensions={0}, use_global_device_ids=true | all-gather | bytes 110592 | tf_op jit(solution)/shard_map/all_gather | solution.py:56
  183.7 0.1 reshape.191
  183.8 0.6 gather_fusion.1
  184.4 0.6 gather_fusion.3
  184.9 0.6 gather_fusion.2
  185.5 0.1 multiply_reduce_fusion.1
  185.6 0.6 broadcast_multiply_fusion.1
  186.2 0.3 fusion.19
  186.5 0.3 convolution_add_fusion
  186.8 0.3 fusion.17
  187.1 4.2 multiply_convert_fusion
  191.2 13.1 %fusion.39 = f32[1024,4096]{1,0:T(8,128)} fusion(bf16[768,1024]{1,0:T(8,128)(2,1)S(1)} %bitcast.80, bf16[768,4096]{1,0:T(8,128)(2,1)} %bitcast.79), kind=kOutput, calls=%fused_computation.83 | convolution fusion | flops 6442450944 | bytes 24641536 | tf_op jit(solution)/shard_map/tj,td->jd/dot_general | solution.py:83
  204.3 0.0 reduce-scatter.2.cloned.1.call-update
  204.3 0.0 all-reduce.3.cloned.1.call-start
  204.4 11.2 %fusion.11 = (f32[4096]{0:T(1024)S(1)}, f32[768]{0:T(1024)S(1)}, f32[768,4096]{1,0:T(8,128)S(1)}) fusion(bf16[1,3,256,4096]{3,2,1,0:T(8,128)(2,1)} %collective-permute-done.1, f32[768]{0:T(1024)S(1)} %rsqrt.16, f32[4096]{0:T(1024)S(1)} %bitcast.85, bf16[768,1024]{1,0:T(8,128)(2,1)S(1)} %bitcast.81, bf16[1024,4096]{1,0:T(8,128)(2,1)} %all-gather.4.cloned.1.call-done), kind=kOutput, calls=%fused_computation.21 | convolution fusion | flops 6464465920 | bytes 28874752 | tf_op jit(solution)/shard_map/dot_general | solution.py:82
  215.6 0.0 copy-start.3
  215.6 8.3 %fusion.8 = bf16[768,4096]{1,0:T(8,128)(2,1)} fusion(bf16[1,3,256,4096]{3,2,1,0:T(8,128)(2,1)} %collective-permute-done.1, f32[768,4096]{1,0:T(8,128)S(1)} %get-tuple-element.18, f32[768]{0:T(1024)S(1)} %broadcast_multiply_fusion, f32[768]{0:T(1024)S(1)} %multiply_multiply_fusion, f32[4096]{0:T(1024)S(1)} %bitcast.86, f32[768]{0:T(1024)S(1)} %rsqrt.16), kind=kLoop, calls=%fused_computation.18 | loop fusion | flops 22020096 | bytes 25191424 | tf_op jit(solution)/shard_map/convert_element_type | solution.py:89
  223.9 259.0 %reduce-scatter.2.cloned.1.call-done = f32[1024,512]{1,0:T(8,128)} async-done(((f32[1024,4096]{1,0:T(8,128)}), f32[1024,512]{1,0:T(8,128)}) %reduce-scatter.2.cloned.1.call-update) | async-done | bytes 2097168 | tf_op jit(solution)/shard_map/reduce_scatter | solution.py:92
  482.9 0.0 all-reduce.3.cloned.1.call-update
  482.9 0.6 dynamic-slice
  484.8 35.2 %all-reduce = f32[4096]{0:T(1024)S(1)} all-reduce(f32[4096]{0:T(1024)S(1)} %get-tuple-element.4), channel_id=3, replica_groups=mesh['section'=4,'fsdp'=8] {'fsdp'}, use_global_device_ids=true, to_apply=%region_9.10.clone | all-reduce | flops 4096 | bytes 32768
  520.0 0.1 dynamic-slice.1
  520.1 7.0 %psum.15 = f32[512]{0:T(512)} all-reduce(f32[512]{0:T(512)S(1)} %dynamic-slice.1), channel_id=1, replica_groups=mesh['section'=4,'fsdp'=8] {'section'}, use_global_device_ids=true, to_apply=%region_10.11 | all-reduce | flops 512 | bytes 4096 | tf_op jit(solution)/shard_map/psum | solution.py:95
  527.1 0.0 collective-permute-done.3
  527.1 8.8 %all-reduce.3.cloned.1.call-done = f32[1024,512]{1,0:T(8,128)} async-done(((f32[1024,512]{1,0:T(8,128)}), f32[1024,512]{1,0:T(8,128)}) %all-reduce.3.cloned.1.call-update) | async-done | bytes 2097168 | tf_op jit(solution)/shard_map/psum | solution.py:95
  535.9 6.4 %copy.25 = bf16[1,3,256,4096]{3,2,1,0:T(8,128)(2,1)} copy(bf16[1,3,256,4096]{3,2,1,0:T(8,128)(2,1)} %collective-permute-done.3) | data formatting | bytes 12582912
  542.3 1.3 copy.26
  (22 shorter events, 0.1 us)
Async XLA Ops:
  7.2 131.6 %all-gather.4.cloned.1.call-start = ((), (), s32[]{:S(2)}) async-start(), calls=%async_computation.1 | async-start | bytes 9437184 | tf_op jit(solution)/shard_map/all_gather | solution.py:35
  10.8 472.1 %reduce-scatter.2.cloned.1.call-start = ((), (), s32[]{:S(2)}) async-start(), calls=%async_computation.2 | async-start | bytes 18874368 | tf_op jit(solution)/shard_map/reduce_scatter | solution.py:92
  10.8 71.7 %collective-permute-start.1 = (bf16[1,3,256,4096]{3,2,1,0:T(8,128)(2,1)}, bf16[1,3,256,4096]{3,2,1,0:T(8,128)(2,1)}, u32[]{:S(2)}, u32[]{:S(2)}) collective-permute-start(bf16[1,3,256,4096]{3,2,1,0:T(8,128)(2,1)} %param.8), channel_id=1, source_target_pairs={{24,0},{0,8},{8,16},{16,24},{25,1},{1,9},{9,17},{17,25},{26,2},{2,... | collective-permute-start | bytes 18874376 | tf_op jit(solution)/shard_map/ppermute | solution.py:20
  11.4 70.9 %collective-permute-start = (s32[1,3]{1,0:T(1,128)}, s32[1,3]{1,0:T(1,128)S(1)}, u32[]{:S(2)}, u32[]{:S(2)}) collective-permute-start(s32[1,3]{1,0:T(1,128)} %param.9), channel_id=1, source_target_pairs={{24,0},{0,8},{8,16},{16,24},{25,1},{1,9},{9,17},{17,25},{26,2},{2,... | collective-permute-start | bytes 44 | tf_op jit(solution)/shard_map/ppermute | solution.py:20
  13.9 68.4 %collective-permute-start.2 = (s32[1,3,4]{2,0,1:T(1,128)}, s32[1,3,4]{2,0,1:T(1,128)S(1)}, u32[]{:S(2)}, u32[]{:S(2)}) collective-permute-start(s32[1,3,4]{2,0,1:T(1,128)} %param.10), channel_id=1, source_target_pairs={{24,0},{0,8},{8,16},{16,24},{25,1},{1,9},{9,17},{17,25},{26,2},{2,... | collective-permute-start | bytes 152 | tf_op jit(solution)/shard_map/ppermute | solution.py:20
  94.9 90.8 %copy-start.2 = (f32[1,8]{1,0:T(1,128)S(1)}, f32[1,8]{1,0:T(1,128)}, u32[]{:S(2)}) copy-start(f32[1,8]{1,0:T(1,128)} %param.13) | copy-start | bytes 100
  150.0 3.0 copy-start
  204.3 331.5 %all-reduce.3.cloned.1.call-start = ((), (), s32[]{:S(2)}) async-start(), calls=%async_computation.3 | async-start | bytes 4194304 | tf_op jit(solution)/shard_map/psum | solution.py:95
  215.6 267.3 %copy-start.3 = (u32[32]{0:T(128)S(1)}, u32[32]{0:T(128)}, u32[]{:S(2)}) copy-start(u32[32]{0:T(128)} %constant.39) | copy-start | bytes 388
  223.9 303.2 %collective-permute-start.3 = (bf16[1,3,256,4096]{3,2,1,0:T(8,128)(2,1)}, bf16[1,3,256,4096]{3,2,1,0:T(8,128)(2,1)}, u32[]{:S(2)}, u32[]{:S(2)}) collective-permute-start(bf16[1,3,256,4096]{3,2,1,0:T(8,128)(2,1)} %bitcast.17), channel_id=1, source_target_pairs={{8,0},{16,8},{24,16},{0,24},{9,1},{17,9},{25,17},{1,25},{10,2},{18... | collective-permute-start | bytes 18874376 | tf_op jit(solution)/shard_map/ppermute | solution.py:20
  535.9 6.4 %copy-start.1 = (f32[1024,512]{1,0:T(8,128)S(1)}, f32[1024,512]{1,0:T(8,128)}, u32[]{:S(2)}) copy-start(f32[1024,512]{1,0:T(8,128)} %all-reduce.3.cloned.1.call-done) | copy-start | bytes 6291460
Sparse Core Ops, SparseCore 0:
  10.9 127.8 all-gather.3
  204.4 278.3 reduce-scatter.1
  485.2 50.5 all-reduce.2
where the time goes:
time: 552 us; the launch traced here: 551 us
  waiting for transfers between devices  352 us (64%)
  blocking collectives  99.8 us (18%)
  matrix products  36.3 us (7%)
  other arithmetic  29.4 us (5%)
  between operations  16.3 us (3%)
  local copies, waits for them, and re-layouts  14.5 us (3%)
    reduce_scatter x1, waiting for transfers between devices, local(): lax.psum_scatter(head_part, 'fsdp', scatter_dimension=1, tiled=True)  259 us
    all_gather x1, waiting for transfers between devices, local(): lax.all_gather(local_rows, 'fsdp', axis=1, tiled=True)  43.9 us
    ppermute x4, waiting for transfers between devices, passed_along(): return lax.ppermute(block, axis, route)  39.9 us
    unnamed x1, blocking collectives  35.2 us
    all_gather x1, blocking collectives, local(): all_pooled = lax.all_gather(pooled, 'fsdp', axis=0, tiled=True)  30.7 us
    all_gather x1, blocking collectives, local(): lax.all_gather(norm_gain, 'fsdp', axis=0, tiled=True)  26.9 us
    dot_general x1, matrix products, local(): jnp.einsum('tj,td->jd', grad_logits, normed, preferred_element_type=jnp.f...  13.1 us
    dot_general x1, matrix products, local(): jnp.einsum('td,jd->tj', normed, window, preferred_element_type=jnp.float32)  11.2 us
  transfers between devices with their start and end apart: 7, of which 4 were waited for; matrix products, arithmetic and copies ran while one was open for 6% of the time, Pallas kernels for 0%

commit v1 on v0

--- a/solution.py
+++ b/solution.py
@@ -26,22 +26,29 @@
 
 
 def local(produced, lengths, active, window_blocks, triplets, teacher, norm_gain, head):
-    hidden, seq_lengths, block_slots = passed_along((produced, lengths, active), "section", 1)
+    sections, shards = lax.axis_size("section"), lax.axis_size("fsdp")
+    group_data = jnp.concatenate([triplets[0].astype(jnp.float32), teacher[0][:, None]], axis=1)
+    group_data = passed_along(group_data, "section", -1)
+    triplet_rows = group_data[:, :3].astype(jnp.int32)
+    target = group_data[:, 3]
     columns = head.shape[1]
-    local_rows = head.reshape(head.shape[0] // BLOCK, BLOCK, columns)[window_blocks].reshape(
-        U * BLOCK, columns
+    own_blocks = U // sections
+    block_ids = lax.dynamic_slice(
+        window_blocks, (lax.axis_index("section") * own_blocks,), (own_blocks,)
     )
-    window, gain_full = (
-        lax.all_gather(local_rows, "fsdp", axis=1, tiled=True),
-        lax.all_gather(norm_gain, "fsdp", axis=0, tiled=True),
+    local_rows = head.reshape(head.shape[0] // BLOCK, BLOCK, columns)[block_ids].reshape(
+        own_blocks * BLOCK, columns
     )
+    piece = lax.all_gather(local_rows, "fsdp", axis=1, tiled=True)
+    window = lax.all_gather(piece, "section", axis=0, tiled=True)
+    gain_full = lax.all_gather(norm_gain, "fsdp", axis=0, tiled=True)
     gain32 = gain_full.astype(jnp.float32)
-    tokens = hidden.reshape(SEQ_DEV * LEN, D)
+    tokens = produced.reshape(SEQ_DEV * LEN, D)
     widened = tokens.astype(jnp.float32)
     inv_rms = lax.rsqrt(jnp.mean(widened * widened, axis=1, keepdims=True) + eps)
     normed = (widened * inv_rms * gain32).astype(jnp.bfloat16)
-    seq_len_row = seq_lengths[0]
-    slot_table = block_slots[0]
+    seq_len_row = lengths[0]
+    slot_table = active[0]
     position = jnp.arange(LEN, dtype=jnp.int32)
     weight = (position[None, :] < seq_len_row[:, None]).astype(jnp.float32) / seq_len_row[
         :, None
@@ -54,13 +61,12 @@
     values, slopes = pool_terms(logits.reshape(SEQ_DEV, LEN, U * BLOCK))
     pooled = jnp.sum(weight[:, :, None] * values, axis=1) * spread
     all_pooled = lax.all_gather(pooled, "fsdp", axis=0, tiled=True)
-    triplet_rows = triplets[0]
     query_rows = all_pooled[triplet_rows[:, 0]]
     positive = all_pooled[triplet_rows[:, 1]]
     negative = all_pooled[triplet_rows[:, 2]]
     margin = jnp.sum(query_rows * (positive - negative), axis=1)
-    deviation = margin - teacher[0]
-    loss_value = jnp.mean(deviation * deviation)
+    deviation = margin - target
+    loss_value = passed_along(jnp.mean(deviation * deviation).reshape(1), "section", 1)
     grad_margin = loss_scale * 2.0 * deviation / triplets.shape[1]
     first_row = lax.axis_index("fsdp") * SEQ_DEV
     own_rows = first_row + jnp.arange(SEQ_DEV, dtype=jnp.int32)
@@ -71,29 +77,35 @@
     other_term = grad_margin[:, None] * query_rows
     grad_pooled = jnp.einsum("ts,tj->sj", query_hits, query_term, precision=lax.Precision.HIGHEST)
     grad_pooled = grad_pooled + jnp.einsum(
-        "ts,tj->sj", positive_hits, other_term, precision=lax.Precision.HIGHEST
-    )
-    grad_pooled = grad_pooled - jnp.einsum(
-        "ts,tj->sj", negative_hits, other_term, precision=lax.Precision.HIGHEST
+        "ts,tj->sj", positive_hits - negative_hits, other_term, precision=lax.Precision.HIGHEST
     )
     grad_values = grad_pooled * spread
     grad_logits = (weight[:, :, None] * grad_values[:, None, :] * slopes).astype(jnp.bfloat16)
     grad_logits = grad_logits.reshape(SEQ_DEV * LEN, U * BLOCK)
+    head_part = jnp.einsum(
+        "tj,td->jd", grad_logits, normed, preferred_element_type=jnp.float32
+    ).astype(jnp.bfloat16)
+    rows = U * BLOCK // sections
+    parts = lax.all_to_all(
+        head_part.reshape(sections, rows, D), "section", split_axis=0, concat_axis=0
+    )
+    mine = jnp.sum(parts.astype(jnp.float32), axis=0).astype(jnp.bfloat16)
+    parts = lax.all_to_all(
+        mine.reshape(rows, shards, columns), "fsdp", split_axis=1, concat_axis=0
+    )
+    parts = parts.reshape(shards, rows, columns)
+    mine = jnp.sum(parts.astype(jnp.float32), axis=0).astype(jnp.bfloat16)
+    head_piece = lax.all_gather(mine, "section", axis=0, tiled=True).astype(jnp.float32)
     grad_normed = jnp.dot(grad_logits, window, preferred_element_type=jnp.float32)
-    head_part = jnp.einsum("tj,td->jd", grad_logits, normed, preferred_element_type=jnp.float32)
     gain_part = jnp.sum(grad_normed * widened * inv_rms, axis=0)
     scaled = grad_normed * gain32
     grad_tokens = inv_rms * scaled - widened * (inv_rms * inv_rms * inv_rms) * jnp.mean(
         scaled * widened, axis=1, keepdims=True
     )
     outgoing = grad_tokens.astype(jnp.bfloat16).reshape(1, SEQ_DEV, LEN, D)
-    sent_back = passed_along(outgoing, "section", -1)
-    head_piece, gain_piece = (
-        lax.psum_scatter(head_part, "fsdp", scatter_dimension=1, tiled=True),
-        lax.psum_scatter(gain_part, "fsdp", scatter_dimension=0, tiled=True),
-    )
-    head_piece, gain_piece = lax.psum((head_piece, gain_piece), "section")
-    return (loss_value.reshape(1), sent_back, head_piece, gain_piece)
+    gain_piece = lax.psum_scatter(gain_part, "fsdp", scatter_dimension=0, tiled=True)
+    gain_piece = lax.psum(gain_piece, "section")
+    return (loss_value, outgoing, head_piece, gain_piece)
 
 
 def solution(mesh):

time: 552 us -> 412 us (0.75)
  waiting for transfers between devices: 352 us -> 101 us
  blocking collectives: 99.8 us -> 195 us
  other arithmetic: 29.4 us -> 43 us
    reduce_scatter x1 -> x0, waiting for transfers between devices: 259 us -> none  [local(): lax.psum_scatter(head_part, 'fsdp', scatter_dimension=1, tiled=True)]
    all_to_all x0 -> x1, blocking collectives: none -> 96.9 us  [local(): lax.all_to_all(head_part.reshape(sections, rows, D), 'section', split_axi...]
    ppermute x4 -> x2, waiting for transfers between devices: 39.9 us -> 0.01 us  [passed_along(): return lax.ppermute(block, axis, route)]
    all_to_all x0 -> x1, waiting for transfers between devices: none -> 30 us  [local(): lax.all_to_all(mine.reshape(rows, shards, columns), 'fsdp', split_axis=1,...]
    all_gather x1 -> x3, waiting for transfers between devices: 43.9 us -> 70.9 us  [the longest x1 53.4 us: local(): piece = lax.all_gather(local_rows, 'fsdp', axis=1, tiled=True)]
    psum x1 -> x0, waiting for transfers between devices: 8.79 us -> none  [local(): head_piece, gain_piece = lax.psum((head_piece, gain_piece), 'section')]
    reduce_sum x0 -> x3, other arithmetic: none -> 8.54 us  [the longest x2 7.94 us: local(): mine = jnp.sum(parts.astype(jnp.float32), axis=0).astype(jnp.bfloat16)]
    unnamed x17 -> x15, local copies, waits for them, and re-layouts: 9.92 us -> 2.17 us
  transfers between devices with their start and end apart: 7 -> 6, of which waited for: 4 -> 3; matrix products, arithmetic and copies ran while one was open for 6% -> 10% of each run, Pallas kernels for 0% -> 0%
where the time goes in v1:
time: 412 us; the launch traced here: 411 us
  blocking collectives  195 us (47%)
  waiting for transfers between devices  101 us (25%)
  other arithmetic  43 us (10%)
  matrix products  36.3 us (9%)
  between operations  16.9 us (4%)
  local copies, waits for them, and re-layouts  11.8 us (3%)
  starting transfers between devices  6.99 us (2%)
    all_to_all x1, blocking collectives, local(): lax.all_to_all(head_part.reshape(sections, rows, D), 'section', split_axi...  96.9 us
    all_gather x1, waiting for transfers between devices, local(): piece = lax.all_gather(local_rows, 'fsdp', axis=1, tiled=True)  53.4 us
    unnamed x1, blocking collectives  35.2 us
    all_gather x1, blocking collectives, local(): all_pooled = lax.all_gather(pooled, 'fsdp', axis=0, tiled=True)  30.8 us
    all_to_all x1, waiting for transfers between devices, local(): lax.all_to_all(mine.reshape(rows, shards, columns), 'fsdp', split_axis=1,...  30 us
    all_gather x1, blocking collectives, local(): gain_full = lax.all_gather(norm_gain, 'fsdp', axis=0, tiled=True)  26.1 us
    all_gather x1, waiting for transfers between devices, local(): window = lax.all_gather(piece, 'section', axis=0, tiled=True)  17.4 us
    dot_general x1, matrix products, local(): jnp.dot(grad_logits, window, preferred_element_type=jnp.float32)  14.1 us
  transfers between devices with their start and end apart: 6, of which 3 were waited for; matrix products, arithmetic and copies ran while one was open for 10% of the time, Pallas kernels for 0%

profile of v1, /device:TPU:0, one launch (start us, length us, event | category | flops | bytes accessed | tf_op | source)
XLA Modules:
  0.0 411.1 jit_solution(8364398150087656315)
XLA Ops:
  7.2 0.0 all-gather.6.cloned.1.call-start
  7.2 0.7 compare_select_fusion.3
  8.0 2.2 gather_fusion
  10.2 0.0 all-gather.6.cloned.1.call-update
  10.2 0.0 all-gather.8.cloned.1.call-start
  10.3 53.4 %all-gather.6.cloned.1.call-done = bf16[256,4096]{1,0:T(8,128)(2,1)} async-done(((bf16[256,512]{1,0:T(8,128)(2,1)}), bf16[256,4096]{1,0:T(8,128)(2,1)}) %all-gather.6.cloned.1.call-update) | async-done | bytes 2097168 | tf_op jit(solution)/shard_map/all_gather | solution.py:42
  63.7 0.7 convert_element_type.86
  64.4 0.7 pad_maximum_fusion
  65.1 0.2 collective-permute-start
  65.3 0.7 copy.27
  65.9 0.7 reshape.187
  66.6 26.1 %all-gather = bf16[8,1,512]{2,1,0:T(2,128)(2,1)S(1)} all-gather(bf16[1,1,512]{2,1,0:T(2,128)(2,1)S(1)} %reshape.187), channel_id=1, replica_groups=mesh['section'=4,'fsdp'=8] {'fsdp'}, dimensions={0}, use_global_device_ids=true | all-gather | bytes 9216 | tf_op jit(solution)/shard_map/all_gather | solution.py:44
  92.8 0.1 convert_reduce_fusion
  92.9 0.8 bitcast_convert_fusion
  93.7 0.9 convert_divide_fusion
  94.6 4.1 %fusion.3 = f32[3,256]{1,0:T(4,128)S(1)} fusion(bf16[1,3,256,4096]{3,2,1,0:T(8,128)(2,1)} %param.8), kind=kLoop, calls=%fused_computation.13 | loop fusion | flops 9436416 | bytes 6294528 | tf_op jit(solution)/shard_map/reduce_sum | solution.py:48
  98.7 0.1 broadcast_bitcast_fusion
  98.8 5.4 %fusion.5 = bf16[1,3,256,4096]{3,2,1,0:T(8,128)(2,1)} fusion(bf16[1,3,256,4096]{3,2,1,0:T(8,128)(2,1)S(1)} %copy-done, f32[4096]{0:T(1024)S(1)} %bitcast.97, f32[3,256]{1,0:T(4,128)S(1)} %add_rsqrt_fusion), kind=kLoop, calls=%fused_computation.15 | loop fusion | flops 12582912 | bytes 12602368 | tf_op jit(solution)/shard_map/convert_element_type | solution.py:49
  104.3 17.4 %all-gather.8.cloned.1.call-done = bf16[1024,4096]{1,0:T(8,128)(2,1)} async-done(((bf16[256,4096]{1,0:T(8,128)(2,1)}), bf16[1024,4096]{1,0:T(8,128)(2,1)}) %all-gather.8.cloned.1.call-update) | async-done | bytes 8388624 | tf_op jit(solution)/shard_map/all_gather | solution.py:43
  121.7 11.2 %fusion.18 = (u8[256,1024]{1,0:T(8,128)(4,1)S(1)}, f32[3,256,1024]{2,1,0:T(8,128)S(1)}) fusion(bf16[1024,4096]{1,0:T(8,128)(2,1)} %all-gather.8.cloned.1.call-done, bf16[1,3,256,4096]{3,2,1,0:T(8,128)(2,1)} %param.8, f32[4096]{0:T(1024)S(1)} %bitcast.98, f32[3,256]{1,0:T(4,128)S(1)} %add_rsqrt_fusion), kind=kOutput, calls=%fused_computation.34 | convolution fusion | flops 6458703872 | bytes 18107392 | tf_op jit(solution)/shard_map/td,jd->tj/dot_general | solution.py:60
  133.0 3.0 multiply_reduce_fusion
  136.0 30.8 %all-gather.1 = f32[8,3,1024]{2,1,0:T(4,128)S(1)} all-gather(f32[1,3,1024]{2,1,0:T(4,128)S(1)} %fusion.22), channel_id=1, replica_groups=mesh['section'=4,'fsdp'=8] {'fsdp'}, dimensions={0}, use_global_device_ids=true | all-gather | bytes 110592 | tf_op jit(solution)/shard_map/all_gather | solution.py:63
  166.7 0.1 reshape.190
  166.8 0.6 gather_fusion.1
  167.4 0.6 gather_fusion.3
  167.9 0.6 gather_fusion.2
  168.5 0.1 multiply_reduce_fusion.1
  168.6 0.3 fusion.19
  169.0 0.3 fusion.17
  169.2 3.7 multiply_convert_fusion
  172.9 10.4 %convolution_convert_fusion = bf16[1024,4096]{1,0:T(8,128)(2,1)S(1)} fusion(bf16[768,1024]{1,0:T(8,128)(2,1)S(1)} %bitcast.94, bf16[768,4096]{1,0:T(8,128)(2,1)} %bitcast.92), kind=kOutput, calls=%fused_computation.24 | convolution fusion | flops 6446645248 | bytes 16252928 | tf_op jit(solution)/shard_map/tj,td->jd/dot_general | solution.py:85
  183.3 96.9 %all_to_all.14 = bf16[4,256,4096]{2,1,0:T(8,128)(2,1)} all-to-all(bf16[4,256,4096]{2,1,0:T(8,128)(2,1)S(1)} %bitcast.90), channel_id=1, replica_groups=mesh['section'=4,'fsdp'=8] {'section'}, dimensions={0} | all-to-all | bytes 16777216 | tf_op jit(solution)/shard_map/all_to_all | solution.py:89
  280.2 6.9 %reduce_sum.96 = bf16[256,4096]{1,0:T(8,128)(2,1)} reduce(bf16[4,256,4096]{2,1,0:T(8,128)(2,1)} %all_to_all.14, bf16[]{:T(256)} %constant.44.clone.1), dimensions={0}, to_apply=%region_6.7 | reduce | flops 3145728 | bytes 10485762 | tf_op jit(solution)/shard_map/reduce_sum | solution.py:92
  287.1 3.3 copy.15
  290.4 2.4 copy.16
  292.8 5.4 %all-to-all-start.1 = ((bf16[1,256,8,512]{3,1,0,2:T(8,128)(2,1)}), bf16[1,256,8,512]{3,1,0,2:T(8,128)(2,1)S(1)}, u32[]{:S(2)}, u32[]{:S(2)}) async-start(bf16[1,256,8,512]{3,1,0,2:T(8,128)(2,1)} %copy.16), calls=%async_computation.1 | async-start | bytes 4194304 | tf_op jit(solution)/shard_map/all_to_all | solution.py:93
  298.2 0.0 all-gather.10.cloned.1.call-start
  298.3 0.6 dynamic-slice
  299.5 0.6 fusion.42
  300.8 1.2 collective-permute-start.1
  302.0 14.1 %fusion.11 = (f32[4096]{0:T(1024)S(1)}, f32[768]{0:T(1024)S(1)}, f32[768,4096]{1,0:T(8,128)}) fusion(bf16[1,3,256,4096]{3,2,1,0:T(8,128)(2,1)} %param.8, f32[768]{0:T(1024)S(1)} %rsqrt.16, f32[4096]{0:T(1024)S(1)} %bitcast.99, bf16[768,1024]{1,0:T(8,128)(2,1)} %bitcast.95, bf16[1024,4096]{1,0:T(8,128)(2,1)} %all-gather.8.cloned.1.call-done), kind=kOutput, calls=%fused_computation.21 | convolution fusion | flops 6464465920 | bytes 28874752 | tf_op jit(solution)/shard_map/dot_general | solution.py:99
  316.1 30.0 %all-to-all-done.1 = bf16[1,256,8,512]{3,1,0,2:T(8,128)(2,1)S(1)} async-done(((bf16[1,256,8,512]{3,1,0,2:T(8,128)(2,1)}), bf16[1,256,8,512]{3,1,0,2:T(8,128)(2,1)S(1)}, u32[]{:S(2)}, u32[]{:S(2)}) %all-to-all-start.1) | async-done | bytes 2097184 | tf_op jit(solution)/shard_map/all_to_all | solution.py:93
  346.1 1.0 reduce_sum.97
  347.2 35.2 %all-reduce = f32[4096]{0:T(1024)S(1)} all-reduce(f32[4096]{0:T(1024)S(1)} %get-tuple-element.4), channel_id=2, replica_groups=mesh['section'=4,'fsdp'=8] {'fsdp'}, use_global_device_ids=true, to_apply=%region_9.10.clone | all-reduce | flops 4096 | bytes 32768
  382.4 0.1 dynamic-slice.1
  382.5 6.2 %psum.7 = f32[512]{0:T(512)} all-reduce(f32[512]{0:T(512)S(1)} %dynamic-slice.1), channel_id=1, replica_groups=mesh['section'=4,'fsdp'=8] {'section'}, use_global_device_ids=true, to_apply=%region_10.11 | all-reduce | flops 512 | bytes 4096 | tf_op jit(solution)/shard_map/psum | solution.py:107
  388.7 11.4 %fusion.8 = bf16[768,4096]{1,0:T(8,128)(2,1)} fusion(bf16[1,3,256,4096]{3,2,1,0:T(8,128)(2,1)} %param.8, f32[768,4096]{1,0:T(8,128)} %get-tuple-element.16, f32[768]{0:T(1024)S(1)} %broadcast_multiply_fusion, f32[768]{0:T(1024)S(1)} %multiply_multiply_fusion, f32[4096]{0:T(1024)S(1)} %bitcast.100, f32[768]{0:T(1024)S(1)} %rsqrt.16), kind=kLoop, calls=%fused_computation.18 | loop fusion | flops 22020096 | bytes 25191424 | tf_op jit(solution)/shard_map/convert_element_type | solution.py:105
  400.0 2.8 convert_element_type.98
  (27 shorter events, 0.2 us)
Async XLA Ops:
  7.2 56.5 %all-gather.6.cloned.1.call-start = ((), (), s32[]{:S(2)}) async-start(), calls=%async_computation.2 | async-start | bytes 2359296 | tf_op jit(solution)/shard_map/all_gather | solution.py:42
  10.2 111.5 %all-gather.8.cloned.1.call-start = ((), (), s32[]{:S(2)}) async-start(), calls=%async_computation.3 | async-start | bytes 10485760 | tf_op jit(solution)/shard_map/all_gather | solution.py:43
  65.1 39.2 %collective-permute-start = (f32[8,4]{0,1:T(4,128)S(1)}, f32[8,4]{0,1:T(4,128)S(1)}, u32[]{:S(2)}, u32[]{:S(2)}) collective-permute-start(f32[8,4]{0,1:T(4,128)S(1)} %pad_maximum_fusion), channel_id=1, source_target_pairs={{8,0},{16,8},{24,16},{0,24},{9,1},{17,9},{25,17},{1,25},{10,2},{18... | collective-permute-start | bytes 392 | tf_op jit(solution)/shard_map/ppermute | solution.py:20
  92.8 6.1 %copy-start = (bf16[1,3,256,4096]{3,2,1,0:T(8,128)(2,1)S(1)}, bf16[1,3,256,4096]{3,2,1,0:T(8,128)(2,1)}, u32[]{:S(2)}) copy-start(bf16[1,3,256,4096]{3,2,1,0:T(8,128)(2,1)} %param.8) | copy-start | bytes 18874372
  133.0 3.0 copy-start.2
  172.9 10.4 %copy-start.1 = (bf16[3,256,1024]{2,1,0:T(8,128)(2,1)}, bf16[3,256,1024]{2,1,0:T(8,128)(2,1)S(1)}, u32[]{:S(2)}) copy-start(bf16[3,256,1024]{2,1,0:T(8,128)(2,1)S(1)} %multiply_convert_fusion) | copy-start | bytes 4718596
  287.1 11.2 %copy-start.3 = (u32[32]{0:T(128)S(1)}, u32[32]{0:T(128)}, u32[]{:S(2)}) copy-start(u32[32]{0:T(128)} %constant.52) | copy-start | bytes 388
  292.8 53.3 %all-to-all-start.1 = ((bf16[1,256,8,512]{3,1,0,2:T(8,128)(2,1)}), bf16[1,256,8,512]{3,1,0,2:T(8,128)(2,1)S(1)}, u32[]{:S(2)}, u32[]{:S(2)}) async-start(bf16[1,256,8,512]{3,1,0,2:T(8,128)(2,1)} %copy.16), calls=%async_computation.1 | async-start | bytes 4194304 | tf_op jit(solution)/shard_map/all_to_all | solution.py:93
  298.2 101.8 %all-gather.10.cloned.1.call-start = ((), (), s32[]{:S(2)}) async-start(), calls=%async_computation.4 | async-start | bytes 1310720 | tf_op jit(solution)/shard_map/all_gather | solution.py:98
  300.8 99.2 %collective-permute-start.1 = (f32[1]{0:T(128)}, f32[1]{0:T(128)}, u32[]{:S(2)}, u32[]{:S(2)}) collective-permute-start(f32[1]{0:T(128)} %bitcast.12), channel_id=1, source_target_pairs={{24,0},{0,8},{8,16},{16,24},{25,1},{1,9},{9,17},{17,25},{26,2},{2,... | collective-permute-start | bytes 20 | tf_op jit(solution)/shard_map/ppermute | solution.py:20
Sparse Core Ops, SparseCore 0:
  10.6 53.0 all-gather.5
  65.2 56.4 all-gather.7
  347.3 15.0 all-gather.9

commit v2 on v1

--- a/solution.py
+++ b/solution.py
@@ -1,6 +1,8 @@
 import jax
 import jax.numpy as jnp
 from jax import lax
+from jax.experimental import pallas as pl
+from jax.experimental.pallas import tpu as pltpu
 from jax.sharding import PartitionSpec as P
 
 D = 4096
@@ -23,6 +25,300 @@
 def pool_terms(logits):
     smooth = jax.nn.softplus(logits)
     return (jnp.log1p(smooth), jax.nn.sigmoid(logits) / (1.0 + smooth))
+
+
+MESH = pl.DeviceIdType.MESH
+VMEM = pl.BlockSpec(memory_space=pltpu.VMEM)
+ANY = pl.BlockSpec(memory_space=pl.ANY)
+bf16, f32 = jnp.bfloat16, jnp.float32
+
+
+def place():
+    s, f = lax.axis_index("section"), lax.axis_index("fsdp")
+    mate = s + 1 - 2 * lax.rem(s, 2)
+    across = lax.rem(s + 2, 4)
+    return s, f, mate, across
+
+
+def greet(others):
+    barrier = pltpu.get_barrier_semaphore()
+    for device in others:
+        pl.semaphore_signal(barrier, inc=1, device_id=device, device_id_type=MESH)
+    pl.semaphore_wait(barrier, len(others))
+
+
+def remote(src, dst, send, recv, device):
+    return pltpu.make_async_remote_copy(
+        src_ref=src,
+        dst_ref=dst,
+        send_sem=send,
+        recv_sem=recv,
+        device_id=device,
+        device_id_type=MESH,
+    )
+
+
+def gather_kernel(n, piece_ref, gain_ref, window_ref, gains_ref, send, recv, gsend, grecv, own_sem):
+    s, f, mate, across = place()
+    lines = n // 2
+    a, b = lax.div(f, 2), lax.rem(f, 2)
+    rows, columns = piece_ref.shape
+    peers = [(s, lax.rem(f + d, n)) for d in range(1, n)]
+    greet(peers + [(mate, f), (across, f)])
+    sent = []
+
+    def region(q, g):
+        return window_ref.at[
+            pl.ds(pl.multiple_of(q * rows, rows), rows),
+            pl.ds(pl.multiple_of(g * columns, columns), columns),
+        ]
+
+    def push(src, q, g, index, device):
+        copy = remote(src, region(q, g), send.at[index], recv.at[index], device)
+        copy.start()
+        sent.append(copy)
+
+    def arrive(q, g, index):
+        spot = region(q, g)
+        remote(spot, spot, send.at[index], recv.at[index], (mate, f)).wait_recv()
+        return spot
+
+    side = lambda d: 2 * lax.rem(a - d + lines, lines) + b
+    other = lambda d: 2 * lax.rem(a - d + lines, lines) + 1 - b
+    to_y, to_x, to_mate, to_last = lines, 2 * lines, 4 * lines, 6 * lines
+
+    def spread_out(src, g, d, half):
+        push(src, s, g, to_x + half * lines + d, (across, f))
+        push(src, s, g, to_mate + half * lines + d, (mate, f))
+
+    for d in range(1, lines):
+        push(piece_ref, s, f, d, (s, 2 * lax.rem(a + d, lines) + b))
+    push(piece_ref, s, f, to_y, (s, 2 * a + 1 - b))
+    spread_out(piece_ref, f, 0, 0)
+    own = pltpu.make_async_copy(piece_ref, region(s, f), own_sem)
+    own.start()
+    gain_copies = []
+    for d in range(1, n):
+        copy = remote(gain_ref, gains_ref.at[f], gsend.at[d], grecv.at[d], peers[d - 1])
+        copy.start()
+        gain_copies.append(copy)
+    gains_ref[f] = gain_ref[...]
+    spread_out(arrive(s, other(0), to_y), other(0), 0, 1)
+    for d in range(1, lines):
+        spot = arrive(s, side(d), d)
+        push(spot, s, side(d), to_y + d, (s, 2 * a + 1 - b))
+        spread_out(spot, side(d), d, 0)
+    for d in range(1, lines):
+        spread_out(arrive(s, other(d), to_y + d), other(d), d, 1)
+    order = [(0, 0), (0, 1)] + [(d, 0) for d in range(1, lines)] + [(d, 1) for d in range(1, lines)]
+    name = lambda d, half: other(d) if half else side(d)
+    for d, half in order:
+        spot = arrive(across, name(d, half), to_x + half * lines + d)
+        push(spot, across, name(d, half), to_last + half * lines + d, (mate, f))
+    mate_across = lax.rem(mate + 2, 4)
+    for d, half in order:
+        arrive(mate, name(d, half), to_mate + half * lines + d)
+        arrive(mate_across, name(d, half), to_last + half * lines + d)
+    for d in range(1, n):
+        spot = gains_ref.at[lax.rem(f - d + n, n)]
+        remote(spot, spot, gsend.at[d], grecv.at[d], peers[d - 1]).wait_recv()
+    own.wait()
+    for copy in sent + gain_copies:
+        copy.wait_send()
+
+
+def gather_window(piece, gain, n):
+    rows, columns = piece.shape
+    count = 8 * (n // 2)
+    return pl.pallas_call(
+        lambda *refs: gather_kernel(n, *refs),
+        name="gather_window",
+        out_shape=(
+            jax.ShapeDtypeStruct((4 * rows, n * columns), bf16),
+            jax.ShapeDtypeStruct((n, 1, columns), f32),
+        ),
+        in_specs=[VMEM, VMEM],
+        out_specs=(ANY, VMEM),
+        scratch_shapes=[
+            pltpu.SemaphoreType.DMA((count,)),
+            pltpu.SemaphoreType.DMA((count,)),
+            pltpu.SemaphoreType.DMA((n,)),
+            pltpu.SemaphoreType.DMA((n,)),
+            pltpu.SemaphoreType.DMA,
+        ],
+        compiler_params=pltpu.CompilerParams(collective_id=0, has_side_effects=True),
+    )(piece, gain)
+
+
+def pool_kernel(n, in_ref, out_ref, send, recv):
+    s, f, _, _ = place()
+    peers = [(s, lax.rem(f + d, n)) for d in range(1, n)]
+    greet(peers)
+    copies = []
+    for d in range(1, n):
+        copy = remote(in_ref, out_ref.at[f], send.at[d], recv.at[d], peers[d - 1])
+        copy.start()
+        copies.append(copy)
+    out_ref[f] = in_ref[...]
+    for d in range(1, n):
+        spot = out_ref.at[lax.rem(f - d + n, n)]
+        remote(spot, spot, send.at[d], recv.at[d], peers[d - 1]).wait_recv()
+    for copy in copies:
+        copy.wait_send()
+
+
+def gather_pooled(pooled, n):
+    return pl.pallas_call(
+        lambda *refs: pool_kernel(n, *refs),
+        name="gather_pooled",
+        out_shape=jax.ShapeDtypeStruct((n,) + pooled.shape, f32),
+        in_specs=[VMEM],
+        out_specs=VMEM,
+        scratch_shapes=[pltpu.SemaphoreType.DMA((n,)), pltpu.SemaphoreType.DMA((n,))],
+        compiler_params=pltpu.CompilerParams(collective_id=1, has_side_effects=True),
+    )(pooled)
+
+
+def reduce_kernel(
+    n, part_ref, gain_ref, out_ref, gain_out,
+    got_mate, sum_x, got_x, sum_y, got_y, sum_z, got_z, final, got_gain, gain_sum, got_sum,
+    send_a, recv_a, send_x, recv_x, send_y, recv_y, send_z, recv_z, send_o, recv_o,
+    gsend, grecv, ssend, srecv,
+):
+    s, f, mate, across = place()
+    lines = n // 2
+    a, b = lax.div(f, 2), lax.rem(f, 2)
+    rows, columns = final.shape
+    diagonal = lax.rem(mate + 2, 4)
+    peers = [(s, lax.rem(f + d, n)) for d in range(1, n)]
+    sections = [(lax.rem(s + d, 4), f) for d in range(1, 4)]
+    greet(peers + sections)
+    sent = []
+
+    def push(src, dst, send, recv, device):
+        copy = remote(src, dst, send, recv, device)
+        copy.start()
+        sent.append(copy)
+
+    def arrive(spot, send, recv):
+        remote(spot, spot, send, recv, (mate, f)).wait_recv()
+
+    chunk = [lax.rem(a + 1 + d, lines) for d in range(lines)]
+
+    def band(q):
+        return pl.ds(pl.multiple_of(q * rows, rows), rows)
+
+    def span(d):
+        return pl.ds(pl.multiple_of(chunk[d] * 2 * columns, 2 * columns), 2 * columns)
+
+    def half_span(d, half):
+        return pl.ds(
+            pl.multiple_of((chunk[d] * 2 + half) * columns, columns), columns
+        )
+
+    def half(h):
+        return pl.ds(pl.multiple_of(h * columns, columns), columns)
+
+    for d in range(lines):
+        for k, q in ((0, diagonal), (1, mate)):
+            push(
+                part_ref.at[band(q), span(d)], got_mate.at[d, k],
+                send_a.at[d, k], recv_a.at[d, k], (mate, f),
+            )
+    for d in range(1, n):
+        device = peers[d - 1]
+        push(gain_ref.at[device[1]], got_gain.at[d], gsend.at[d], grecv.at[d], device)
+    for d in range(lines):
+        arrive(got_mate.at[d, 0], send_a.at[d, 0], recv_a.at[d, 0])
+        sum_x[d] = (
+            part_ref[band(across), span(d)].astype(f32) + got_mate[d, 0].astype(f32)
+        ).astype(bf16)
+        push(sum_x.at[d], got_x.at[d], send_x.at[d], recv_x.at[d], (across, f))
+    total = gain_ref[f]
+    for d in range(1, n):
+        arrive(got_gain.at[d], gsend.at[d], grecv.at[d])
+        total = total + got_gain[d]
+    gain_sum[...] = total
+    for d in range(1, 4):
+        push(gain_sum, got_sum.at[d], ssend.at[d], srecv.at[d], sections[d - 1])
+
+    def gathered(d, h):
+        return (
+            part_ref[band(s), half_span(d, h)].astype(f32)
+            + got_mate[d, 1, :, half(h)].astype(f32)
+            + got_x[d, :, half(h)].astype(f32)
+        )
+
+    def finish(d):
+        arrive(got_y.at[d], send_y.at[d], recv_y.at[d])
+        value = gathered(d, b) + got_y[d].astype(f32)
+        if d < lines - 1:
+            sum_z[d] = value.astype(bf16)
+            push(sum_z.at[d], got_z.at[d], send_z.at[d], recv_z.at[d], (s, 2 * chunk[d] + b))
+        return value
+
+    for d in range(lines):
+        arrive(got_mate.at[d, 1], send_a.at[d, 1], recv_a.at[d, 1])
+        arrive(got_x.at[d], send_x.at[d], recv_x.at[d])
+        sum_y[d] = gathered(d, 1 - b).astype(bf16)
+        push(sum_y.at[d], got_y.at[d], send_y.at[d], recv_y.at[d], (s, 2 * a + 1 - b))
+        if d > 0:
+            finish(d - 1)
+    value = finish(lines - 1)
+    for d in range(lines - 1):
+        arrive(got_z.at[d], send_z.at[d], recv_z.at[d])
+        value = value + got_z[d].astype(f32)
+    final[...] = value.astype(bf16)
+    push(final, out_ref.at[band(s)], send_o.at[0], recv_o.at[0], (across, f))
+    push(final, out_ref.at[band(s)], send_o.at[1], recv_o.at[1], (mate, f))
+    out_ref[band(s), :] = value.astype(bf16)
+    for d in range(1, 4):
+        arrive(got_sum.at[d], ssend.at[d], srecv.at[d])
+    gain_out[...] = gain_sum[...] + got_sum[1] + got_sum[2] + got_sum[3]
+    arrive(out_ref.at[band(across)], send_o.at[0], recv_o.at[0])
+    push(
+        out_ref.at[band(across)], out_ref.at[band(across)],
+        send_o.at[2], recv_o.at[2], (mate, f),
+    )
+    arrive(out_ref.at[band(mate)], send_o.at[1], recv_o.at[1])
+    arrive(out_ref.at[band(diagonal)], send_o.at[2], recv_o.at[2])
+    for copy in sent:
+        copy.wait_send()
+
+
+def reduce_head(part, gain, n):
+    terms, width = part.shape
+    rows, columns, lines = terms // 4, width // n, n // 2
+    sems = [pltpu.SemaphoreType.DMA((lines, 2))] * 2 + [pltpu.SemaphoreType.DMA((lines,))] * 6
+    sems += [pltpu.SemaphoreType.DMA((3,))] * 2 + [pltpu.SemaphoreType.DMA((n,))] * 2
+    sems += [pltpu.SemaphoreType.DMA((4,))] * 2
+    return pl.pallas_call(
+        lambda *refs: reduce_kernel(n, *refs),
+        name="reduce_head",
+        out_shape=(
+            jax.ShapeDtypeStruct((terms, columns), bf16),
+            jax.ShapeDtypeStruct((1, columns), f32),
+        ),
+        in_specs=[VMEM, VMEM],
+        out_specs=(VMEM, VMEM),
+        scratch_shapes=[
+            pltpu.VMEM((lines, 2, rows, 2 * columns), bf16),
+            pltpu.VMEM((lines, rows, 2 * columns), bf16),
+            pltpu.VMEM((lines, rows, 2 * columns), bf16),
+            pltpu.VMEM((lines, rows, columns), bf16),
+            pltpu.VMEM((lines, rows, columns), bf16),
+            pltpu.VMEM((lines, rows, columns), bf16),
+            pltpu.VMEM((lines, rows, columns), bf16),
+            pltpu.VMEM((rows, columns), bf16),
+            pltpu.VMEM((n, 1, columns), f32),
+            pltpu.VMEM((1, columns), f32),
+            pltpu.VMEM((4, 1, columns), f32),
+        ]
+        + sems,
+        compiler_params=pltpu.CompilerParams(
+            collective_id=2, has_side_effects=True, vmem_limit_bytes=56 << 20
+        ),
+    )(part, gain)
 
 
 def local(produced, lengths, active, window_blocks, triplets, teacher, norm_gain, head):
@@ -39,10 +335,9 @@
     local_rows = head.reshape(head.shape[0] // BLOCK, BLOCK, columns)[block_ids].reshape(
         own_blocks * BLOCK, columns
     )
-    piece = lax.all_gather(local_rows, "fsdp", axis=1, tiled=True)
-    window = lax.all_gather(piece, "section", axis=0, tiled=True)
-    gain_full = lax.all_gather(norm_gain, "fsdp", axis=0, tiled=True)
-    gain32 = gain_full.astype(jnp.float32)
+    gain_own = norm_gain.astype(jnp.float32)[None, :]
+    window, gains = gather_window(local_rows, gain_own, shards)
+    gain32 = gains.reshape(D)
     tokens = produced.reshape(SEQ_DEV * LEN, D)
     widened = tokens.astype(jnp.float32)
     inv_rms = lax.rsqrt(jnp.mean(widened * widened, axis=1, keepdims=True) + eps)
@@ -60,7 +355,7 @@
     logits = jnp.einsum("td,jd->tj", normed, window, preferred_element_type=jnp.float32)
     values, slopes = pool_terms(logits.reshape(SEQ_DEV, LEN, U * BLOCK))
     pooled = jnp.sum(weight[:, :, None] * values, axis=1) * spread
-    all_pooled = lax.all_gather(pooled, "fsdp", axis=0, tiled=True)
+    all_pooled = gather_pooled(pooled, shards).reshape(shards * SEQ_DEV, U * BLOCK)
     query_rows = all_pooled[triplet_rows[:, 0]]
     positive = all_pooled[triplet_rows[:, 1]]
     negative = all_pooled[triplet_rows[:, 2]]
@@ -85,17 +380,6 @@
     head_part = jnp.einsum(
         "tj,td->jd", grad_logits, normed, preferred_element_type=jnp.float32
     ).astype(jnp.bfloat16)
-    rows = U * BLOCK // sections
-    parts = lax.all_to_all(
-        head_part.reshape(sections, rows, D), "section", split_axis=0, concat_axis=0
-    )
-    mine = jnp.sum(parts.astype(jnp.float32), axis=0).astype(jnp.bfloat16)
-    parts = lax.all_to_all(
-        mine.reshape(rows, shards, columns), "fsdp", split_axis=1, concat_axis=0
-    )
-    parts = parts.reshape(shards, rows, columns)
-    mine = jnp.sum(parts.astype(jnp.float32), axis=0).astype(jnp.bfloat16)
-    head_piece = lax.all_gather(mine, "section", axis=0, tiled=True).astype(jnp.float32)
     grad_normed = jnp.dot(grad_logits, window, preferred_element_type=jnp.float32)
     gain_part = jnp.sum(grad_normed * widened * inv_rms, axis=0)
     scaled = grad_normed * gain32
@@ -103,8 +387,9 @@
         scaled * widened, axis=1, keepdims=True
     )
     outgoing = grad_tokens.astype(jnp.bfloat16).reshape(1, SEQ_DEV, LEN, D)
-    gain_piece = lax.psum_scatter(gain_part, "fsdp", scatter_dimension=0, tiled=True)
-    gain_piece = lax.psum(gain_piece, "section")
+    head_piece, gain_piece = reduce_head(head_part, gain_part.reshape(shards, 1, columns), shards)
+    head_piece = head_piece.astype(jnp.float32)
+    gain_piece = gain_piece.reshape(columns)
     return (loss_value, outgoing, head_piece, gain_piece)
 
 

time: 412 us -> 242 us (0.59)
  blocking collectives: 195 us -> 0 us
  Pallas kernels: 0 us -> 145 us
  waiting for transfers between devices: 101 us -> 0.01 us
  between operations: 16.9 us -> 3.23 us
  local copies, waits for them, and re-layouts: 11.8 us -> 7.19 us
    pallas_call x0 -> x3, Pallas kernels: none -> 145 us  [the longest x1 74.1 us: reduce_head(): pl.pallas_call(lambda *refs: reduce_kernel(n, *refs), name='reduce_head',...]
    all_to_all x1 -> x0, blocking collectives: 96.9 us -> none  [local(): lax.all_to_all(head_part.reshape(sections, rows, D), 'section', split_axi...]
    all_gather x3 -> x0, waiting for transfers between devices: 70.9 us -> none  [the longest x1 53.4 us: local(): piece = lax.all_gather(local_rows, 'fsdp', axis=1, tiled=True)]
    all_gather x2 -> x0, blocking collectives: 56.9 us -> none  [the longest x1 30.8 us: local(): all_pooled = lax.all_gather(pooled, 'fsdp', axis=0, tiled=True)]
    unnamed x1 -> x0, blocking collectives: 35.2 us -> none
    all_to_all x1 -> x0, waiting for transfers between devices: 30 us -> none  [local(): lax.all_to_all(mine.reshape(rows, shards, columns), 'fsdp', split_axis=1,...]
    reduce_sum x2 -> x0, other arithmetic: 7.94 us -> none  [local(): mine = jnp.sum(parts.astype(jnp.float32), axis=0).astype(jnp.bfloat16)]
    psum x1 -> x0, blocking collectives: 6.2 us -> none  [local(): gain_piece = lax.psum(gain_piece, 'section')]
  transfers between devices with their start and end apart: 6 -> 2, of which waited for: 3 -> 0; matrix products, arithmetic and copies ran while one was open for 10% -> 33% of each run, Pallas kernels for 0% -> 60%
where the time goes in v2:
time: 242 us; the launch traced here: 241 us
  Pallas kernels  145 us (60%)
  other arithmetic  45.6 us (19%)
  matrix products  37.1 us (15%)
  local copies, waits for them, and re-layouts  7.19 us (3%)
  starting transfers between devices  3.6 us (1%)
  between operations  3.23 us (1%)
    pallas_call x1, Pallas kernels, reduce_head(): pl.pallas_call(lambda *refs: reduce_kernel(n, *refs), name='reduce_head',...  74.1 us
    pallas_call x1, Pallas kernels, gather_window(): pl.pallas_call(lambda *refs: gather_kernel(n, *refs), name='gather_window...  57.1 us
    dot_general x1, matrix products, local(): jnp.dot(grad_logits, window, preferred_element_type=jnp.float32)  15.6 us
    pallas_call x1, Pallas kernels, gather_pooled(): pl.pallas_call(lambda *refs: pool_kernel(n, *refs), name='gather_pooled',...  13.4 us
    dot_general x1, matrix products, local(): jnp.einsum('td,jd->tj', normed, window, preferred_element_type=jnp.float32)  10.5 us
    convert_element_type x1, other arithmetic, local(): outgoing = grad_tokens.astype(jnp.bfloat16).reshape(1, SEQ_DEV, LEN, D)  10.2 us
    dot_general x1, matrix products, local(): jnp.einsum('tj,td->jd', grad_logits, normed, preferred_element_type=jnp.f...  9 us
    convert_element_type x1, other arithmetic, local(): normed = (widened * inv_rms * gain32).astype(jnp.bfloat16)  8.18 us
  transfers between devices with their start and end apart: 2, of which 0 were waited for; matrix products, arithmetic and copies ran while one was open for 33% of the time, Pallas kernels for 60%

profile of v2, /device:TPU:0, one launch (start us, length us, event | category | flops | bytes accessed | tf_op | source)
XLA Modules:
  0.0 241.3 jit_solution(12362923214991231105)
XLA Ops:
  0.6 0.7 convert_element_type.79
  1.3 1.2 pad_maximum_fusion
  2.6 2.4 collective-permute-start
  5.0 0.7 compare_select_fusion.3
  5.7 1.3 broadcast_in_dim.12
  7.0 4.1 %fusion.3 = f32[3,256]{1,0:T(4,128)S(1)} fusion(bf16[1,3,256,4096]{3,2,1,0:T(8,128)(2,1)} %param.8), kind=kLoop, calls=%fused_computation.13 | loop fusion | flops 9436416 | bytes 6294528 | tf_op jit(solution)/shard_map/reduce_sum | solution.py:343
  11.1 2.2 gather_fusion
  13.3 57.1 %gather_window.1 = (bf16[1024,4096]{1,0:T(8,128)(2,1)}, f32[8,1,512]{2,1,0:T(1,128)}) custom-call(bf16[256,512]{1,0:T(8,128)(2,1)} %bitcast.96, f32[1,512]{1,0:T(1,128)} %bitcast.102), custom_call_target="tpu_custom_call" | custom-call | tf_op jit(solution)/shard_map/gather_window/pallas_call | solution.py:133
  70.4 0.0 slice-start.1
  70.4 8.2 %fusion.5 = bf16[1,3,256,4096]{3,2,1,0:T(8,128)(2,1)} fusion(bf16[1,3,256,4096]{3,2,1,0:T(8,128)(2,1)} %param.8, f32[4096]{0:T(1024)} %bitcast.97, f32[3,256]{1,0:T(4,128)S(1)} %add_rsqrt_fusion), kind=kLoop, calls=%fused_computation.15 | loop fusion | flops 12582912 | bytes 12602368 | tf_op jit(solution)/shard_map/convert_element_type | solution.py:344
  78.6 0.0 copy-start.9
  78.6 0.0 copy-start.8
  78.7 10.5 %fusion.18 = (u8[256,1024]{1,0:T(8,128)(4,1)S(1)}, f32[3,256,1024]{2,1,0:T(8,128)}) fusion(bf16[1024,4096]{1,0:T(8,128)(2,1)} %get-tuple-element.9, bf16[1,3,256,4096]{3,2,1,0:T(8,128)(2,1)S(1)} %bitcast.87, f32[4096]{0:T(1024)S(1)} %bitcast.98, f32[3,256]{1,0:T(4,128)S(1)} %add_rsqrt_fusion), kind=kOutput, calls=%fused_computation.34 | convolution fusion | flops 6458703872 | bytes 18107392 | tf_op jit(solution)/shard_map/td,jd->tj/dot_general | solution.py:355
  89.2 0.0 copy-done.9
  89.2 0.0 copy-start
  89.2 0.1 convert_reduce_fusion
  89.3 0.1 broadcast_bitcast_fusion
  89.4 0.5 iota_add_fusion
  89.9 0.6 multiply_multiply_fusion
  90.5 0.1 convert_divide_fusion
  90.6 4.9 %multiply_reduce_fusion = f32[3,1024]{1,0:T(4,128)S(1)} fusion(f32[3,256,1024]{2,1,0:T(8,128)} %get-tuple-element.23, f32[3,256]{1,0:T(4,128)S(1)} %convert_divide_fusion, u8[256,1024]{1,0:T(8,128)(4,1)S(1)} %get-tuple-element.22), kind=kLoop, calls=%fused_computation.30 | loop fusion | flops 8647680 | bytes 3423232 | tf_op jit(solution)/shard_map/reduce_sum | solution.py:357
  95.4 0.6 bitcast_multiply_fusion.3.refs_0_
  96.0 13.4 %gather_pooled.1 = f32[8,3,1024]{2,1,0:T(4,128)} custom-call(f32[3,1024]{1,0:T(4,128)} %bitcast_multiply_fusion.3.refs_0_), custom_call_target="tpu_custom_call" | custom-call | tf_op jit(solution)/shard_map/gather_pooled/pallas_call | solution.py:171
  109.5 1.0 reshape.154
  110.4 0.0 collective-permute-done
  110.5 0.7 slice_convert_fusion
  111.1 0.6 slice_bitcast_fusion.2
  111.7 0.0 copy-done.2
  111.7 0.6 pad_clamp_fusion.2
  112.3 0.7 gather_fusion.1
  113.0 1.3 pad_clamp_fusion
  114.3 1.3 gather_fusion.2
  115.6 1.3 gather_fusion.3
  116.9 0.9 multiply_reduce_fusion.1
  117.8 1.3 fusion.41
  119.7 1.2 collective-permute-start.1
  120.9 0.7 fusion.39
  121.6 1.0 fusion.19
  122.6 1.0 fusion.17
  123.6 0.0 slice-start.4
  123.6 3.6 %multiply_convert_fusion = bf16[3,256,1024]{2,1,0:T(8,128)(2,1)S(1)} fusion(f32[3,256,1024]{2,1,0:T(8,128)S(1)} %copy-done, f32[3,1024]{1,0:T(4,128)S(1)} %fusion.17, f32[3,256]{1,0:T(4,128)} %copy-done.5, u8[256,1024]{1,0:T(8,128)(4,1)S(1)} %get-tuple-element.22), kind=kLoop, calls=%fused_computation.29 | loop fusion | flops 13369344 | bytes 4996096 | tf_op jit(solution)/shard_map/convert_element_type | solution.py:378
  127.2 0.0 slice-start.5
  127.2 15.6 %fusion.11 = (f32[4096]{0:T(1024)}, f32[768]{0:T(1024)S(1)}, f32[768,4096]{1,0:T(8,128)}) fusion(bf16[1,3,256,4096]{3,2,1,0:T(8,128)(2,1)} %param.8, f32[768]{0:T(1024)} %copy-done.3, f32[4096]{0:T(1024)S(1)} %bitcast.99, bf16[768,1024]{1,0:T(8,128)(2,1)S(1)} %bitcast.94, bf16[1024,4096]{1,0:T(8,128)(2,1)} %get-tuple-element.9), kind=kOutput, calls=%fused_computation.21 | convolution fusion | flops 6464465920 | bytes 28874752 | tf_op jit(solution)/shard_map/dot_general | solution.py:383
  142.8 9.0 %convolution_convert_fusion.refs_0_ = bf16[1024,4096]{1,0:T(8,128)(2,1)} fusion(bf16[768,1024]{1,0:T(8,128)(2,1)S(1)} %bitcast.95, bf16[768,4096]{1,0:T(8,128)(2,1)S(1)} %bitcast.92), kind=kOutput, calls=%fused_computation.24 | convolution fusion | flops 6446645248 | bytes 16252928 | tf_op jit(solution)/shard_map/tj,td->jd/dot_general | solution.py:380
  151.8 74.1 %reduce_head.1 = (bf16[1024,512]{1,0:T(8,128)(2,1)}, f32[1,512]{1,0:T(1,128)}) custom-call(bf16[1024,4096]{1,0:T(8,128)(2,1)} %convolution_convert_fusion.refs_0_, f32[8,1,512]{2,1,0:T(1,128)} %bitcast.101), custom_call_target="tpu_custom_call" | custom-call | tf_op jit(solution)/shard_map/reduce_head/pallas_call | solution.py:295
  225.9 2.8 %convert_element_type.91 = f32[1024,512]{1,0:T(8,128)} convert(bf16[1024,512]{1,0:T(8,128)(2,1)} %get-tuple-element.10) | non-fusion elementwise | flops 524288 | bytes 3145728 | tf_op jit(solution)/shard_map/convert_element_type | solution.py:391
  228.8 10.2 %fusion.8 = bf16[768,4096]{1,0:T(8,128)(2,1)} fusion(bf16[1,3,256,4096]{3,2,1,0:T(8,128)(2,1)S(1)} %bitcast.89, f32[768,4096]{1,0:T(8,128)} %get-tuple-element.24, f32[768]{0:T(1024)S(1)} %broadcast_multiply_fusion, f32[768]{0:T(1024)S(1)} %copy-done.6, f32[4096]{0:T(1024)S(1)} %bitcast.100, f32[768]{0:T(1024)S(1)} %copy-done.4), kind=kLoop, calls=%fused_computation.18 | loop fusion | flops 22020096 | bytes 25191424 | tf_op jit(solution)/shard_map/convert_element_type | solution.py:389
  239.6 0.6 copy.24
  (35 shorter events, 0.1 us)
Async XLA Ops:
  2.6 107.9 %collective-permute-start = (f32[8,4]{0,1:T(4,128)}, f32[8,4]{0,1:T(4,128)}, u32[]{:S(2)}, u32[]{:S(2)}) collective-permute-start(f32[8,4]{0,1:T(4,128)} %pad_maximum_fusion), channel_id=1, source_target_pairs={{8,0},{16,8},{24,16},{0,24},{9,1},{17,9},{25,17},{1,25},{10,2},{18... | collective-permute-start | bytes 392 | tf_op jit(solution)/shard_map/ppermute | solution.py:22
  11.1 78.8 %copy-start.3 = (f32[768]{0:T(1024)}, f32[768]{0:T(1024)S(1)}, u32[]{:S(2)}) copy-start(f32[768]{0:T(1024)S(1)} %rsqrt.16) | copy-start | bytes 9220
  13.3 65.3 %slice-start = ((s8[6291456]{0:T(1024)(128)(4,1)}), s8[2097152]{0:T(1024)(128)(4,1)S(1)}, s32[]{:S(2)}) async-start(s8[6291456]{0:T(1024)(128)(4,1)} %bitcast.86), calls=%async_computation | async-start | bytes 4194304
  70.4 8.2 %slice-start.1 = ((s8[6291456]{0:T(1024)(128)(4,1)}), s8[4194304]{0:T(1024)(128)(4,1)S(1)}, s32[]{:S(2)}) async-start(s8[6291456]{0:T(1024)(128)(4,1)} %bitcast.86), calls=%async_computation.1 | async-start | bytes 8388608
  70.4 8.2 %copy-start.1 = (f32[8,1,512]{2,1,0:T(1,128)S(1)}, f32[8,1,512]{2,1,0:T(1,128)}, u32[]{:S(2)}) copy-start(f32[8,1,512]{2,1,0:T(1,128)} %get-tuple-element.8) | copy-start | bytes 49156
  78.6 10.5 %copy-start.9 = (s32[1,3]{1,0:T(1,128)S(1)}, s32[1,3]{1,0:T(1,128)}, u32[]{:S(2)}) copy-start(s32[1,3]{1,0:T(1,128)} %param.9) | copy-start | bytes 40
  78.6 10.6 %copy-start.8 = (s32[1,3,4]{2,0,1:T(1,128)S(1)}, s32[1,3,4]{2,0,1:T(1,128)}, u32[]{:S(2)}) copy-start(s32[1,3,4]{2,0,1:T(1,128)} %param.10) | copy-start | bytes 148
  89.2 34.4 %copy-start = (f32[3,256,1024]{2,1,0:T(8,128)S(1)}, f32[3,256,1024]{2,1,0:T(8,128)}, u32[]{:S(2)}) copy-start(f32[3,256,1024]{2,1,0:T(8,128)} %get-tuple-element.23) | copy-start | bytes 9437188
  89.4 22.4 %copy-start.2 = (f32[1,3,8,128]{3,2,1,0:T(8,128)}, f32[1,3,8,128]{3,2,1,0:T(8,128)S(1)}, u32[]{:S(2)}) copy-start(f32[1,3,8,128]{3,2,1,0:T(8,128)S(1)} %broadcast_bitcast_fusion) | copy-start | bytes 36868
  90.6 21.2 %copy-start.5 = (f32[3,256]{1,0:T(4,128)}, f32[3,256]{1,0:T(4,128)S(1)}, u32[]{:S(2)}) copy-start(f32[3,256]{1,0:T(4,128)S(1)} %convert_divide_fusion) | copy-start | bytes 9220
  119.7 119.3 %collective-permute-start.1 = (f32[1]{0:T(128)}, f32[1]{0:T(128)}, u32[]{:S(2)}, u32[]{:S(2)}) collective-permute-start(f32[1]{0:T(128)} %bitcast.12), channel_id=1, source_target_pairs={{24,0},{0,8},{8,16},{16,24},{25,1},{1,9},{9,17},{17,25},{26,2},{2,... | collective-permute-start | bytes 20 | tf_op jit(solution)/shard_map/ppermute | solution.py:22
  123.6 19.2 %slice-start.4 = ((s8[6291456]{0:T(1024)(128)(4,1)}), s8[4194304]{0:T(1024)(128)(4,1)S(1)}, s32[]{:S(2)}) async-start(s8[6291456]{0:T(1024)(128)(4,1)} %bitcast.90), calls=%async_computation.4 | async-start | bytes 8388608
  127.2 15.6 %slice-start.5 = ((s8[6291456]{0:T(1024)(128)(4,1)}), s8[2097152]{0:T(1024)(128)(4,1)S(1)}, s32[]{:S(2)}) async-start(s8[6291456]{0:T(1024)(128)(4,1)} %bitcast.90), calls=%async_computation.5 | async-start | bytes 4194304
  151.8 76.9 %slice-start.2 = ((s8[6291456]{0:T(1024)(128)(4,1)}), s8[4194304]{0:T(1024)(128)(4,1)S(1)}, s32[]{:S(2)}) async-start(s8[6291456]{0:T(1024)(128)(4,1)} %bitcast.88), calls=%async_computation.2 | async-start | bytes 8388608
  151.8 76.9 %copy-start.4 = (f32[768]{0:T(1024)S(1)}, f32[768]{0:T(1024)}, u32[]{:S(2)}) copy-start(f32[768]{0:T(1024)} %copy-done.3) | copy-start | bytes 9220
  151.8 76.9 %copy-start.6 = (f32[768]{0:T(1024)S(1)}, f32[768]{0:T(1024)}, u32[]{:S(2)}) copy-start(f32[768]{0:T(1024)} %multiply_multiply_fusion) | copy-start | bytes 9220
  151.8 76.9 %slice-start.3 = ((s8[6291456]{0:T(1024)(128)(4,1)}), s8[2097152]{0:T(1024)(128)(4,1)S(1)}, s32[]{:S(2)}) async-start(s8[6291456]{0:T(1024)(128)(4,1)} %bitcast.88), calls=%async_computation.3 | async-start | bytes 4194304
  228.8 10.8 %copy-start.7 = (f32[1,512]{1,0:T(1,128)S(1)}, f32[1,512]{1,0:T(1,128)}, u32[]{:S(2)}) copy-start(f32[1,512]{1,0:T(1,128)} %get-tuple-element.11) | copy-start | bytes 6148

commit v3 on v2

--- a/solution.py
+++ b/solution.py
@@ -150,37 +150,69 @@
     )(piece, gain)
 
 
-def pool_kernel(n, in_ref, out_ref, send, recv):
+PAD = 8
+
+
+def pick(hits, rows):
+    return jnp.dot(hits, rows, precision=lax.Precision.HIGHEST, preferred_element_type=f32)
+
+
+def pool_kernel(n, in_ref, group_ref, turned_ref, spread_ref, grad_ref, loss_ref, held, send, recv):
     s, f, _, _ = place()
+    trips = group_ref.shape[0]
     peers = [(s, lax.rem(f + d, n)) for d in range(1, n)]
     greet(peers)
     copies = []
     for d in range(1, n):
-        copy = remote(in_ref, out_ref.at[f], send.at[d], recv.at[d], peers[d - 1])
+        copy = remote(in_ref, held.at[f], send.at[d], recv.at[d], peers[d - 1])
         copy.start()
         copies.append(copy)
-    out_ref[f] = in_ref[...]
-    for d in range(1, n):
-        spot = out_ref.at[lax.rem(f - d + n, n)]
+    held[f] = in_ref[...]
+    names = lax.broadcasted_iota(jnp.int32, (trips, n * PAD), 1).astype(f32)
+    group = group_ref[...]
+    hits = [(names == group[:, k : k + 1]).astype(f32) for k in range(3)]
+    own = (lax.broadcasted_iota(jnp.int32, (PAD, trips), 0) + f * PAD).astype(f32)
+    turned = turned_ref[...]
+    own_hits = [(own == turned[k : k + 1, :]).astype(f32) for k in range(3)]
+    for d in range(1, n):
+        spot = held.at[lax.rem(f - d + n, n)]
         remote(spot, spot, send.at[d], recv.at[d], peers[d - 1]).wait_recv()
+    rows = held[...].reshape(n * PAD, held.shape[2])
+    query = pick(hits[0], rows)
+    gap = pick(hits[1], rows) - pick(hits[2], rows)
+    deviation = jnp.sum(query * gap, axis=1, keepdims=True) - group[:, 3:4]
+    loss = jnp.sum(deviation * deviation, axis=0, keepdims=True) / trips
+    loss_ref[...] = jnp.broadcast_to(loss, loss_ref.shape)
+    grad_margin = loss_scale * 2.0 * deviation / trips
+    grad = pick(own_hits[0], grad_margin * gap)
+    grad = grad + pick(own_hits[1] - own_hits[2], grad_margin * query)
+    grad_ref[...] = grad * spread_ref[...]
     for copy in copies:
         copy.wait_send()
 
 
-def gather_pooled(pooled, n):
+def pooled_grads(pooled, group, spread, n):
     return pl.pallas_call(
         lambda *refs: pool_kernel(n, *refs),
-        name="gather_pooled",
-        out_shape=jax.ShapeDtypeStruct((n,) + pooled.shape, f32),
-        in_specs=[VMEM],
-        out_specs=VMEM,
-        scratch_shapes=[pltpu.SemaphoreType.DMA((n,)), pltpu.SemaphoreType.DMA((n,))],
+        name="pooled_grads",
+        out_shape=(
+            jax.ShapeDtypeStruct(pooled.shape, f32),
+            jax.ShapeDtypeStruct((1, 128), f32),
+        ),
+        in_specs=[VMEM] * 4,
+        out_specs=(VMEM, VMEM),
+        scratch_shapes=[
+            pltpu.VMEM((n,) + pooled.shape, f32),
+            pltpu.SemaphoreType.DMA((n,)),
+            pltpu.SemaphoreType.DMA((n,)),
+        ],
         compiler_params=pltpu.CompilerParams(collective_id=1, has_side_effects=True),
-    )(pooled)
+    )(pooled, group, group.T, spread)
 
 
 def reduce_kernel(
-    n, part_ref, gain_ref, out_ref, gain_out,
+    n, part_ref, logit_ref, window_hbm, token_hbm, inv_ref, norm_ref, out_ref, gain_out, grad_hbm,
+    window_ref, token_ref, grad_ref, product, gain_row, gain_ref, load_sem, store_sem,
     got_mate, sum_x, got_x, sum_y, got_y, sum_z, got_z, final, got_gain, gain_sum, got_sum,
     send_a, recv_a, send_x, recv_x, send_y, recv_y, send_z, recv_z, send_o, recv_o,
     gsend, grecv, ssend, srecv,
@@ -225,22 +257,55 @@
                 part_ref.at[band(q), span(d)], got_mate.at[d, k],
                 send_a.at[d, k], recv_a.at[d, k], (mate, f),
             )
-    for d in range(1, n):
-        device = peers[d - 1]
-        push(gain_ref.at[device[1]], got_gain.at[d], gsend.at[d], grecv.at[d], device)
+    loads = [
+        pltpu.make_async_copy(window_hbm, window_ref, load_sem.at[0]),
+        pltpu.make_async_copy(token_hbm, token_ref, load_sem.at[1]),
+    ]
+    for load in loads:
+        load.start()
     for d in range(lines):
         arrive(got_mate.at[d, 0], send_a.at[d, 0], recv_a.at[d, 0])
         sum_x[d] = (
             part_ref[band(across), span(d)].astype(f32) + got_mate[d, 0].astype(f32)
         ).astype(bf16)
         push(sum_x.at[d], got_x.at[d], send_x.at[d], recv_x.at[d], (across, f))
-    total = gain_ref[f]
-    for d in range(1, n):
-        arrive(got_gain.at[d], gsend.at[d], grecv.at[d])
-        total = total + got_gain[d]
-    gain_sum[...] = total
-    for d in range(1, 4):
-        push(gain_sum, got_sum.at[d], ssend.at[d], srecv.at[d], sections[d - 1])
+    for load in loads:
+        load.wait()
+    gain_row[...] = jnp.zeros_like(gain_row)
+    height, width = product.shape
+    tile = width // 4
+
+    def store(i):
+        own = pl.ds(pl.multiple_of(i * height, height), height)
+        return pltpu.make_async_copy(grad_ref.at[own], grad_hbm.at[own], store_sem.at[i])
+
+    def token_block(i, carry):
+        own = pl.ds(pl.multiple_of(i * height, height), height)
+        inv = inv_ref[own, :]
+        dots = jnp.zeros((height, 1), f32)
+        for c in range(4):
+            cols = slice(c * tile, (c + 1) * tile)
+            grad = jnp.dot(logit_ref[own, :], window_ref[:, cols], preferred_element_type=f32)
+            wide = token_ref[own, cols].astype(f32)
+            gain_row[:, cols] += jnp.sum(grad * wide * inv, axis=0, keepdims=True)
+            scaled = grad * norm_ref[:, cols]
+            product[:, cols] = scaled
+            dots = dots + jnp.sum(scaled * wide, axis=1, keepdims=True)
+        factor = inv * inv * inv * (dots / width)
+        for c in range(4):
+            cols = slice(c * tile, (c + 1) * tile)
+            wide = token_ref[own, cols].astype(f32)
+            grad_ref[own, cols] = (inv * product[:, cols] - wide * factor).astype(bf16)
+        store(i).start()
+        return carry
+
+    blocks = token_ref.shape[0] // height
+    lax.fori_loop(0, blocks, token_block, 0)
+    for g in range(n):
+        gain_ref[g] = gain_row[:, g * columns : (g + 1) * columns]
+    for d in range(1, n):
+        device = peers[d - 1]
+        push(gain_ref.at[device[1]], got_gain.at[d], gsend.at[d], grecv.at[d], device)
 
     def gathered(d, h):
         return (
@@ -264,6 +329,13 @@
         push(sum_y.at[d], got_y.at[d], send_y.at[d], recv_y.at[d], (s, 2 * a + 1 - b))
         if d > 0:
             finish(d - 1)
+    total = gain_ref[f]
+    for d in range(1, n):
+        arrive(got_gain.at[d], gsend.at[d], grecv.at[d])
+        total = total + got_gain[d]
+    gain_sum[...] = total
+    for d in range(1, 4):
+        push(gain_sum, got_sum.at[d], ssend.at[d], srecv.at[d], sections[d - 1])
     value = finish(lines - 1)
     for d in range(lines - 1):
         arrive(got_z.at[d], send_z.at[d], recv_z.at[d])
@@ -282,12 +354,15 @@
     )
     arrive(out_ref.at[band(mate)], send_o.at[1], recv_o.at[1])
     arrive(out_ref.at[band(diagonal)], send_o.at[2], recv_o.at[2])
+    for i in range(blocks):
+        store(i).wait()
     for copy in sent:
         copy.wait_send()
 
 
-def reduce_head(part, gain, n):
+def reduce_head(part, grad_logits, window, tokens, inv_rms, gain, n):
     terms, width = part.shape
+    count = tokens.shape[0]
     rows, columns, lines = terms // 4, width // n, n // 2
     sems = [pltpu.SemaphoreType.DMA((lines, 2))] * 2 + [pltpu.SemaphoreType.DMA((lines,))] * 6
     sems += [pltpu.SemaphoreType.DMA((3,))] * 2 + [pltpu.SemaphoreType.DMA((n,))] * 2
@@ -298,10 +373,19 @@
         out_shape=(
             jax.ShapeDtypeStruct((terms, columns), bf16),
             jax.ShapeDtypeStruct((1, columns), f32),
+            jax.ShapeDtypeStruct(tokens.shape, bf16),
         ),
-        in_specs=[VMEM, VMEM],
-        out_specs=(VMEM, VMEM),
+        in_specs=[VMEM, VMEM, ANY, ANY, VMEM, VMEM],
+        out_specs=(VMEM, VMEM, ANY),
         scratch_shapes=[
+            pltpu.VMEM((terms, width), bf16),
+            pltpu.VMEM((count, width), bf16),
+            pltpu.VMEM((count, width), bf16),
+            pltpu.VMEM((LEN // 2, width), f32),
+            pltpu.VMEM((1, width), f32),
+            pltpu.VMEM((n, 1, columns), f32),
+            pltpu.SemaphoreType.DMA((2,)),
+            pltpu.SemaphoreType.DMA((2 * count // LEN,)),
             pltpu.VMEM((lines, 2, rows, 2 * columns), bf16),
             pltpu.VMEM((lines, rows, 2 * columns), bf16),
             pltpu.VMEM((lines, rows, 2 * columns), bf16),
@@ -316,17 +400,16 @@
         ]
         + sems,
         compiler_params=pltpu.CompilerParams(
-            collective_id=2, has_side_effects=True, vmem_limit_bytes=56 << 20
+            collective_id=2, has_side_effects=True, vmem_limit_bytes=60 << 20
         ),
-    )(part, gain)
+    )(part, grad_logits, window, tokens, inv_rms, gain)
 
 
 def local(produced, lengths, active, window_blocks, triplets, teacher, norm_gain, head):
     sections, shards = lax.axis_size("section"), lax.axis_size("fsdp")
-    group_data = jnp.concatenate([triplets[0].astype(jnp.float32), teacher[0][:, None]], axis=1)
+    places = triplets[0] // SEQ_DEV * PAD + triplets[0] % SEQ_DEV
+    group_data = jnp.concatenate([places.astype(jnp.float32), teacher[0][:, None]], axis=1)
     group_data = passed_along(group_data, "section", -1)
-    triplet_rows = group_data[:, :3].astype(jnp.int32)
-    target = group_data[:, 3]
     columns = head.shape[1]
     own_blocks = U // sections
     block_ids = lax.dynamic_slice(
@@ -355,39 +438,21 @@
     logits = jnp.einsum("td,jd->tj", normed, window, preferred_element_type=jnp.float32)
     values, slopes = pool_terms(logits.reshape(SEQ_DEV, LEN, U * BLOCK))
     pooled = jnp.sum(weight[:, :, None] * values, axis=1) * spread
-    all_pooled = gather_pooled(pooled, shards).reshape(shards * SEQ_DEV, U * BLOCK)
-    query_rows = all_pooled[triplet_rows[:, 0]]
-    positive = all_pooled[triplet_rows[:, 1]]
-    negative = all_pooled[triplet_rows[:, 2]]
-    margin = jnp.sum(query_rows * (positive - negative), axis=1)
-    deviation = margin - target
-    loss_value = passed_along(jnp.mean(deviation * deviation).reshape(1), "section", 1)
-    grad_margin = loss_scale * 2.0 * deviation / triplets.shape[1]
-    first_row = lax.axis_index("fsdp") * SEQ_DEV
-    own_rows = first_row + jnp.arange(SEQ_DEV, dtype=jnp.int32)
-    query_hits = (triplet_rows[:, 0][:, None] == own_rows[None, :]).astype(jnp.float32)
-    positive_hits = (triplet_rows[:, 1][:, None] == own_rows[None, :]).astype(jnp.float32)
-    negative_hits = (triplet_rows[:, 2][:, None] == own_rows[None, :]).astype(jnp.float32)
-    query_term = grad_margin[:, None] * (positive - negative)
-    other_term = grad_margin[:, None] * query_rows
-    grad_pooled = jnp.einsum("ts,tj->sj", query_hits, query_term, precision=lax.Precision.HIGHEST)
-    grad_pooled = grad_pooled + jnp.einsum(
-        "ts,tj->sj", positive_hits - negative_hits, other_term, precision=lax.Precision.HIGHEST
-    )
-    grad_values = grad_pooled * spread
+    padding = ((0, PAD - SEQ_DEV), (0, 0))
+    grad_values, loss_row = pooled_grads(
+        jnp.pad(pooled, padding), group_data, jnp.pad(spread, padding), shards
+    )
+    grad_values = grad_values[:SEQ_DEV]
+    loss_value = passed_along(loss_row[0, :1], "section", 1)
     grad_logits = (weight[:, :, None] * grad_values[:, None, :] * slopes).astype(jnp.bfloat16)
     grad_logits = grad_logits.reshape(SEQ_DEV * LEN, U * BLOCK)
     head_part = jnp.einsum(
         "tj,td->jd", grad_logits, normed, preferred_element_type=jnp.float32
     ).astype(jnp.bfloat16)
-    grad_normed = jnp.dot(grad_logits, window, preferred_element_type=jnp.float32)
-    gain_part = jnp.sum(grad_normed * widened * inv_rms, axis=0)
-    scaled = grad_normed * gain32
-    grad_tokens = inv_rms * scaled - widened * (inv_rms * inv_rms * inv_rms) * jnp.mean(
-        scaled * widened, axis=1, keepdims=True
-    )
-    outgoing = grad_tokens.astype(jnp.bfloat16).reshape(1, SEQ_DEV, LEN, D)
-    head_piece, gain_piece = reduce_head(head_part, gain_part.reshape(shards, 1, columns), shards)
+    head_piece, gain_piece, grad_tokens = reduce_head(
+        head_part, grad_logits, window, tokens, inv_rms, gain32[None, :], shards
+    )
+    outgoing = grad_tokens.reshape(1, SEQ_DEV, LEN, D)
     head_piece = head_piece.astype(jnp.float32)
     gain_piece = gain_piece.reshape(columns)
     return (loss_value, outgoing, head_piece, gain_piece)

time: 242 us -> 218 us (0.901)
  other arithmetic: 45.6 us -> 27.1 us
  matrix products: 37.1 us -> 21.9 us
  local copies, waits for them, and re-layouts: 7.19 us -> 15.2 us
  Pallas kernels: 145 us -> 148 us
    dot_general x3 -> x0, matrix products: 17.6 us -> none  [the longest x1 15.6 us: local(): jnp.dot(grad_logits, window, preferred_element_type=jnp.float32)]
    convert_element_type x3 -> x1, other arithmetic: 11.6 us -> 0.01 us  [local(): places.astype(jnp.float32)]
    unnamed x36 -> x23, local copies, waits for them, and re-layouts: 0.74 us -> 10.3 us
    dot_general x1, matrix products: 9 us -> 12.3 us  [local(): jnp.einsum('tj,td->jd', grad_logits, normed, preferred_element_type=jnp.f...]
    gather x3 -> x0, local copies, waits for them, and re-layouts: 3.26 us -> none  [the longest x1 1.29 us: local(): positive = all_pooled[triplet_rows[:, 1]]]
    pallas_call x1, Pallas kernels: 13.4 us -> 16.1 us  [pooled_grads(): pl.pallas_call(lambda *refs: pool_kernel(n, *refs), name='pooled_grads',...]
  transfers between devices with their start and end apart: 2 -> 2, of which waited for: 0 -> 0; matrix products, arithmetic and copies ran while one was open for 33% -> 24% of each run, Pallas kernels for 60% -> 61%
where the time goes in v3:
time: 218 us
  Pallas kernels  148 us (68%)
  other arithmetic  27.1 us (12%)
  matrix products  21.9 us (10%)
  local copies, waits for them, and re-layouts  15.2 us (7%)
  between operations  2.6 us (1%)
  starting transfers between devices  2.48 us (1%)
    pallas_call x1, Pallas kernels, reduce_head(): pl.pallas_call(lambda *refs: reduce_kernel(n, *refs), name='reduce_head',...  75.2 us
    pallas_call x1, Pallas kernels, gather_window(): pl.pallas_call(lambda *refs: gather_kernel(n, *refs), name='gather_window...  57.1 us
    pallas_call x1, Pallas kernels, pooled_grads(): pl.pallas_call(lambda *refs: pool_kernel(n, *refs), name='pooled_grads',...  16.1 us
    dot_general x1, matrix products, local(): jnp.einsum('tj,td->jd', grad_logits, normed, preferred_element_type=jnp.f...  12.3 us
    unnamed x23, local copies, waits for them, and re-layouts  10.3 us
    dot_general x1, matrix products, local(): jnp.einsum('td,jd->tj', normed, window, preferred_element_type=jnp.float32)  9.53 us
    convert_element_type x1, other arithmetic, local(): normed = (widened * inv_rms * gain32).astype(jnp.bfloat16)  8.18 us
  transfers between devices with their start and end apart: 2, of which 0 were waited for; matrix products, arithmetic and copies ran while one was open for 24% of the time, Pallas kernels for 61%

profile of v3, /device:TPU:0, one launch (start us, length us, event | category | flops | bytes accessed | tf_op | source)
XLA Modules:
  0.0 217.6 jit_solution(3890160025990353827)
XLA Ops:
  0.6 0.7 sign_compare_fusion
  1.3 0.7 broadcast_remainder_fusion
  2.0 0.7 pad_maximum_fusion
  2.7 2.4 %collective-permute-start = (f32[8,4]{0,1:T(4,128)S(1)}, f32[8,4]{0,1:T(4,128)S(1)}, u32[]{:S(2)}, u32[]{:S(2)}) collective-permute-start(f32[8,4]{0,1:T(4,128)S(1)} %pad_maximum_fusion), channel_id=1, source_target_pairs={{8,0},{16,8},{24,16},{0,24},{9,1},{17,9},{25,17},{1,25},{10,2},{18... | collective-permute-start | bytes 392 | tf_op jit(solution)/shard_map/ppermute | solution.py:22
  5.1 0.7 bitcast_convert_fusion
  5.8 0.7 copy.40
  6.4 0.1 convert_reduce_fusion
  6.5 1.3 broadcast_in_dim.21
  7.8 0.7 compare_select_fusion
  8.5 4.1 %fusion.3 = f32[3,256]{1,0:T(4,128)S(1)} fusion(bf16[1,3,256,4096]{3,2,1,0:T(8,128)(2,1)} %param.8), kind=kLoop, calls=%fused_computation.7 | loop fusion | flops 9436416 | bytes 6294528 | tf_op jit(solution)/shard_map/reduce_sum | solution.py:426
  12.6 0.1 broadcast_bitcast_fusion
  12.7 1.0 copy.23
  13.7 2.2 %gather_fusion = bf16[2,128,512]{2,1,0:T(8,128)(2,1)} fusion(bf16[250,128,512]{2,1,0:T(8,128)(2,1)} %bitcast.82, s32[1024]{0:T(1024)S(1)} %pad_clamp_fusion), kind=kCustom, calls=%fused_computation | custom fusion | bytes 524296 | tf_op jit(solution)/shard_map/gather | solution.py:418
  15.9 0.0 slice-start
  15.9 57.1 %gather_window.1 = (bf16[1024,4096]{1,0:T(8,128)(2,1)}, f32[8,1,512]{2,1,0:T(1,128)}) custom-call(bf16[256,512]{1,0:T(8,128)(2,1)} %bitcast.73, f32[1,512]{1,0:T(1,128)} %bitcast.79), custom_call_target="tpu_custom_call" | custom-call | tf_op jit(solution)/shard_map/gather_window/pallas_call | solution.py:133
  73.0 0.0 slice-start.1
  73.0 0.0 copy-start.2
  73.0 8.2 %fusion.5 = bf16[1,3,256,4096]{3,2,1,0:T(8,128)(2,1)} fusion(bf16[1,3,256,4096]{3,2,1,0:T(8,128)(2,1)} %param.8, f32[4096]{0:T(1024)} %bitcast.75, f32[3,256]{1,0:T(4,128)S(1)} %get-tuple-element.19), kind=kLoop, calls=%fused_computation.9 | loop fusion | flops 12582912 | bytes 12602368 | tf_op jit(solution)/shard_map/convert_element_type | solution.py:427
  81.2 0.0 slice-done
  81.2 0.0 slice-done.1
  81.2 0.0 copy-done.2
  81.2 0.0 copy-start.5
  81.2 9.5 %fusion.11 = (u8[256,1024]{1,0:T(8,128)(4,1)S(1)}, f32[3,256,1024]{2,1,0:T(8,128)S(1)}) fusion(bf16[1024,4096]{1,0:T(8,128)(2,1)} %get-tuple-element.12.refs_2_, bf16[1,3,256,4096]{3,2,1,0:T(8,128)(2,1)S(1)} %bitcast.67, f32[4096]{0:T(1024)S(1)} %bitcast.77, f32[3,256]{1,0:T(4,128)S(1)} %get-tuple-element.19), kind=kOutput, calls=%fused_computation.20 | convolution fusion | flops 6458703872 | bytes 18107392 | tf_op jit(solution)/shard_map/td,jd->tj/dot_general | solution.py:438
  90.8 0.0 copy-start.1
  90.8 0.0 copy-done.5
  90.8 0.1 convert_divide_fusion
  90.9 1.6 copy-done.1
  92.5 3.0 %multiply_reduce_fusion = f32[3,1024]{1,0:T(4,128)S(1)} fusion(f32[3,256,1024]{2,1,0:T(8,128)S(1)} %get-tuple-element.23, f32[3,256]{1,0:T(4,128)S(1)} %convert_divide_fusion, u8[256,1024]{1,0:T(8,128)(4,1)S(1)} %get-tuple-element.22), kind=kLoop, calls=%fused_computation.18 | loop fusion | flops 8647680 | bytes 3423232 | tf_op jit(solution)/shard_map/reduce_sum | solution.py:440
  95.5 0.6 pad.8.refs_3_
  96.1 0.6 pad.7.refs_0_
  96.8 0.0 collective-permute-done
  96.8 0.0 copy-start.3
  96.8 0.7 copy.15.refs_1_
  97.4 0.0 copy-done.3
  97.4 16.1 %pooled_grads.1 = (f32[8,1024]{1,0:T(8,128)}, f32[1,128]{1,0:T(1,128)}) custom-call(f32[8,1024]{1,0:T(8,128)} %pad.7.refs_0_, f32[8,4]{1,0:T(8,128)} %copy.15.refs_1_, f32[4,8]{1,0:T(4,128)} %bitcast.80, f32[8,1024]{1,0:T(8,128)} %pad.8.refs_3_), custom_call_target="tpu_custom_call" | custom-call | tf_op jit(solution)/shard_map/pooled_grads/pallas_call | solution.py:195
  113.5 0.1 collective-permute-start.1
  113.6 0.8 slice.7
  114.3 4.2 %multiply_convert_fusion = bf16[3,256,1024]{2,1,0:T(8,128)(2,1)S(1)} fusion(f32[3,256,1024]{2,1,0:T(8,128)} %copy-done.1, f32[3,1024]{1,0:T(4,128)S(1)} %slice.7, f32[3,256]{1,0:T(4,128)S(1)} %convert_divide_fusion, u8[256,1024]{1,0:T(8,128)(4,1)S(1)} %get-tuple-element.22), kind=kLoop, calls=%fused_computation.17 | loop fusion | flops 13369344 | bytes 4996096 | tf_op jit(solution)/shard_map/convert_element_type | solution.py:447
  118.5 0.0 copy-start
  118.5 12.3 %convolution_convert_fusion.refs_0_ = bf16[1024,4096]{1,0:T(8,128)(2,1)} fusion(bf16[768,1024]{1,0:T(8,128)(2,1)S(1)} %bitcast.70, bf16[768,4096]{1,0:T(8,128)(2,1)} %bitcast.68), kind=kOutput, calls=%fused_computation.12 | convolution fusion | flops 6446645248 | bytes 16252928 | tf_op jit(solution)/shard_map/tj,td->jd/dot_general | solution.py:449
  130.8 0.0 copy-done
  130.8 75.2 %reduce_head.1 = (bf16[1024,512]{1,0:T(8,128)(2,1)}, f32[1,512]{1,0:T(1,128)}, bf16[768,4096]{1,0:T(8,128)(2,1)}) custom-call(bf16[1024,4096]{1,0:T(8,128)(2,1)} %convolution_convert_fusion.refs_0_, bf16[768,1024]{1,0:T(8,128)(2,1)} %bitcast.71, bf16[1024,4096]{1,0:T(8,128)(2,1)} %get-tuple-element.12.refs_2_, bf16[768,4096]{1,0:T(8,128)(2,1)} %bitcast.65, ...), custom_call_target="tpu_custom_call" | custom-call | tf_op jit(solution)/shard_map/reduce_head/pallas_call | solution.py:370
  206.1 2.8 %convert_element_type.66 = f32[1024,512]{1,0:T(8,128)} convert(bf16[1024,512]{1,0:T(8,128)(2,1)} %get-tuple-element.16) | non-fusion elementwise | flops 524288 | bytes 3145728 | tf_op jit(solution)/shard_map/convert_element_type | solution.py:456
  208.9 0.0 collective-permute-done.1
  209.6 0.0 copy-start.4
  209.6 6.3 %copy.45 = bf16[1,3,256,4096]{3,2,1,0:T(8,128)(2,1)} copy(bf16[1,3,256,4096]{3,2,1,0:T(8,128)(2,1)} %bitcast.69) | data formatting | bytes 12582912
  215.9 0.0 copy-done.4
  215.9 0.6 copy.46
  (7 shorter events, 0.1 us)
Async XLA Ops:
  2.7 94.1 %collective-permute-start = (f32[8,4]{0,1:T(4,128)S(1)}, f32[8,4]{0,1:T(4,128)S(1)}, u32[]{:S(2)}, u32[]{:S(2)}) collective-permute-start(f32[8,4]{0,1:T(4,128)S(1)} %pad_maximum_fusion), channel_id=1, source_target_pairs={{8,0},{16,8},{24,16},{0,24},{9,1},{17,9},{25,17},{1,25},{10,2},{18... | collective-permute-start | bytes 392 | tf_op jit(solution)/shard_map/ppermute | solution.py:22
  15.9 65.3 %slice-start = ((s8[6291456]{0:T(1024)(128)(4,1)}), s8[2097152]{0:T(1024)(128)(4,1)S(1)}, s32[]{:S(2)}) async-start(s8[6291456]{0:T(1024)(128)(4,1)} %bitcast.66), calls=%async_computation | async-start | bytes 4194304
  73.0 8.2 %slice-start.1 = ((s8[6291456]{0:T(1024)(128)(4,1)}), s8[4194304]{0:T(1024)(128)(4,1)S(1)}, s32[]{:S(2)}) async-start(s8[6291456]{0:T(1024)(128)(4,1)} %bitcast.66), calls=%async_computation.1 | async-start | bytes 8388608
  73.0 8.2 %copy-start.2 = (f32[8,1,512]{2,1,0:T(1,128)S(1)}, f32[8,1,512]{2,1,0:T(1,128)}, u32[]{:S(2)}) copy-start(f32[8,1,512]{2,1,0:T(1,128)} %get-tuple-element.11) | copy-start | bytes 49156
  81.2 9.6 %copy-start.5 = (s32[1,3]{1,0:T(1,128)S(1)}, s32[1,3]{1,0:T(1,128)}, u32[]{:S(2)}) copy-start(s32[1,3]{1,0:T(1,128)} %param.9) | copy-start | bytes 40
  90.8 1.7 copy-start.1
  96.8 0.7 copy-start.3
  113.5 95.4 %collective-permute-start.1 = (f32[1]{0:T(128)}, f32[1]{0:T(128)}, u32[]{:S(2)}, u32[]{:S(2)}) collective-permute-start(f32[1]{0:T(128)} %bitcast.86), channel_id=1, source_target_pairs={{24,0},{0,8},{8,16},{16,24},{25,1},{1,9},{9,17},{17,25},{26,2},{2,... | collective-permute-start | bytes 20 | tf_op jit(solution)/shard_map/ppermute | solution.py:22
  118.5 12.3 %copy-start = (bf16[3,256,1024]{2,1,0:T(8,128)(2,1)}, bf16[3,256,1024]{2,1,0:T(8,128)(2,1)S(1)}, u32[]{:S(2)}) copy-start(bf16[3,256,1024]{2,1,0:T(8,128)(2,1)S(1)} %multiply_convert_fusion) | copy-start | bytes 4718596
  209.6 6.3 %copy-start.4 = (f32[1,512]{1,0:T(1,128)S(1)}, f32[1,512]{1,0:T(1,128)}, u32[]{:S(2)}) copy-start(f32[1,512]{1,0:T(1,128)} %get-tuple-element.17) | copy-start | bytes 6148

commit v4 on v3

--- a/solution.py
+++ b/solution.py
@@ -58,7 +58,10 @@
     )
 
 
-def gather_kernel(n, piece_ref, gain_ref, window_ref, gains_ref, send, recv, gsend, grecv, own_sem):
+def gather_kernel(
+    n, piece_ref, gain_ref, token_hbm, window_ref, gains_ref, normed_ref, inv_ref, logits_ref,
+    token_ref, quarter, send, recv, gsend, grecv, own_sem, token_sem, load_sem,
+):
     s, f, mate, across = place()
     lines = n // 2
     a, b = lax.div(f, 2), lax.rem(f, 2)
@@ -103,32 +106,88 @@
         copy.start()
         gain_copies.append(copy)
     gains_ref[f] = gain_ref[...]
+    width = token_ref.shape[1]
+    blocks = token_ref.shape[0] // LEN
+
+    def rows_of(i):
+        return pl.ds(pl.multiple_of(i * LEN, LEN), LEN)
+
+    def measure_block(i, carry):
+        squares = jnp.zeros((LEN, 1), f32)
+        for g in range(n):
+            wide = token_ref[rows_of(i), g * columns : (g + 1) * columns].astype(f32)
+            squares = squares + jnp.sum(wide * wide, axis=1, keepdims=True)
+        inv_ref[rows_of(i), :] = lax.rsqrt(squares / width + eps)
+        return carry
+
+    def norm_block(i, carry):
+        inv = inv_ref[rows_of(i), :]
+        for g in range(n):
+            cols = slice(g * columns, (g + 1) * columns)
+            wide = token_ref[rows_of(i), cols].astype(f32)
+            normed_ref[rows_of(i), cols] = (wide * inv * gains_ref[g]).astype(bf16)
+        return carry
+
+    def load_quarter(q, k):
+        band = window_ref.at[pl.ds(pl.multiple_of(q * rows, rows), rows)]
+        load = pltpu.make_async_copy(band, quarter.at[k], load_sem.at[k])
+        load.start()
+        return load
+
+    def logits_of(q, k, load):
+        load.wait()
+
+        def block(i, carry):
+            logits_ref[rows_of(i), pl.ds(pl.multiple_of(q * rows, rows), rows)] = lax.dot_general(
+                normed_ref[rows_of(i), :],
+                quarter[k],
+                (((1,), (1,)), ((), ())),
+                preferred_element_type=f32,
+            )
+            return carry
+
+        lax.fori_loop(0, blocks, block, 0)
+
+    tokens = pltpu.make_async_copy(token_hbm, token_ref, token_sem)
+    tokens.start()
+    tokens.wait()
+    lax.fori_loop(0, blocks, measure_block, 0)
     spread_out(arrive(s, other(0), to_y), other(0), 0, 1)
     for d in range(1, lines):
         spot = arrive(s, side(d), d)
         push(spot, s, side(d), to_y + d, (s, 2 * a + 1 - b))
         spread_out(spot, side(d), d, 0)
+    for d in range(1, n):
+        spot = gains_ref.at[lax.rem(f - d + n, n)]
+        remote(spot, spot, gsend.at[d], grecv.at[d], peers[d - 1]).wait_recv()
+    lax.fori_loop(0, blocks, norm_block, 0)
     for d in range(1, lines):
         spread_out(arrive(s, other(d), to_y + d), other(d), d, 1)
     order = [(0, 0), (0, 1)] + [(d, 0) for d in range(1, lines)] + [(d, 1) for d in range(1, lines)]
     name = lambda d, half: other(d) if half else side(d)
+    mate_across = lax.rem(mate + 2, 4)
+    own.wait()
+    own_load = load_quarter(s, 0)
     for d, half in order:
+        arrive(mate, name(d, half), to_mate + half * lines + d)
+    mate_load = load_quarter(mate, 1)
+    logits_of(s, 0, own_load)
+    for k, (d, half) in enumerate(order):
+        if k == len(order) // 2:
+            logits_of(mate, 1, mate_load)
         spot = arrive(across, name(d, half), to_x + half * lines + d)
         push(spot, across, name(d, half), to_last + half * lines + d, (mate, f))
-    mate_across = lax.rem(mate + 2, 4)
+    logits_of(across, 2, load_quarter(across, 2))
     for d, half in order:
-        arrive(mate, name(d, half), to_mate + half * lines + d)
         arrive(mate_across, name(d, half), to_last + half * lines + d)
-    for d in range(1, n):
-        spot = gains_ref.at[lax.rem(f - d + n, n)]
-        remote(spot, spot, gsend.at[d], grecv.at[d], peers[d - 1]).wait_recv()
-    own.wait()
+    logits_of(mate_across, 3, load_quarter(mate_across, 3))
     for copy in sent + gain_copies:
         copy.wait_send()
 
 
-def gather_window(piece, gain, n):
+def gather_window(piece, gain, tokens, n):
     rows, columns = piece.shape
+    tall, width = tokens.shape
     count = 8 * (n // 2)
     return pl.pallas_call(
         lambda *refs: gather_kernel(n, *refs),
@@ -136,18 +195,27 @@
         out_shape=(
             jax.ShapeDtypeStruct((4 * rows, n * columns), bf16),
             jax.ShapeDtypeStruct((n, 1, columns), f32),
+            jax.ShapeDtypeStruct((tall, width), bf16),
+            jax.ShapeDtypeStruct((tall, 1), f32),
+            jax.ShapeDtypeStruct((tall, 4 * rows), f32),
         ),
-        in_specs=[VMEM, VMEM],
-        out_specs=(ANY, VMEM),
+        in_specs=[VMEM, VMEM, ANY],
+        out_specs=(ANY, VMEM, VMEM, VMEM, VMEM),
         scratch_shapes=[
+            pltpu.VMEM((tall, width), bf16),
+            pltpu.VMEM((4, rows, width), bf16),
             pltpu.SemaphoreType.DMA((count,)),
             pltpu.SemaphoreType.DMA((count,)),
             pltpu.SemaphoreType.DMA((n,)),
             pltpu.SemaphoreType.DMA((n,)),
             pltpu.SemaphoreType.DMA,
+            pltpu.SemaphoreType.DMA,
+            pltpu.SemaphoreType.DMA((4,)),
         ],
-        compiler_params=pltpu.CompilerParams(collective_id=0, has_side_effects=True),
-    )(piece, gain)
+        compiler_params=pltpu.CompilerParams(
+            collective_id=0, has_side_effects=True, vmem_limit_bytes=56 << 20
+        ),
+    )(piece, gain, tokens)
 
 
 PAD = 8
@@ -419,12 +487,9 @@
         own_blocks * BLOCK, columns
     )
     gain_own = norm_gain.astype(jnp.float32)[None, :]
-    window, gains = gather_window(local_rows, gain_own, shards)
+    tokens = produced.reshape(SEQ_DEV * LEN, D)
+    window, gains, normed, inv_rms, logits = gather_window(local_rows, gain_own, tokens, shards)
     gain32 = gains.reshape(D)
-    tokens = produced.reshape(SEQ_DEV * LEN, D)
-    widened = tokens.astype(jnp.float32)
-    inv_rms = lax.rsqrt(jnp.mean(widened * widened, axis=1, keepdims=True) + eps)
-    normed = (widened * inv_rms * gain32).astype(jnp.bfloat16)
     seq_len_row = lengths[0]
     slot_table = active[0]
     position = jnp.arange(LEN, dtype=jnp.int32)
@@ -435,7 +500,6 @@
     onehot = (slot_table[:, :, None] == slot_range[None, None, :]).astype(jnp.float32)
     chosen = jnp.sum(onehot, axis=1)
     spread = jnp.repeat(chosen, BLOCK, axis=1)
-    logits = jnp.einsum("td,jd->tj", normed, window, preferred_element_type=jnp.float32)
     values, slopes = pool_terms(logits.reshape(SEQ_DEV, LEN, U * BLOCK))
     pooled = jnp.sum(weight[:, :, None] * values, axis=1) * spread
     padding = ((0, PAD - SEQ_DEV), (0, 0))

time: 218 us -> 202 us (0.927)
  other arithmetic: 27.1 us -> 15.7 us
  matrix products: 21.9 us -> 12.3 us
  Pallas kernels: 148 us -> 155 us
  local copies, waits for them, and re-layouts: 15.2 us -> 12.6 us
    dot_general x1 -> x0, matrix products: 9.53 us -> none  [local(): jnp.einsum('td,jd->tj', normed, window, preferred_element_type=jnp.float32)]
    pallas_call x1, Pallas kernels: 57.1 us -> 66.5 us  [gather_window(): pl.pallas_call(lambda *refs: gather_kernel(n, *refs), name='gather_window...]
    convert_element_type x1 -> x0, other arithmetic: 8.18 us -> none  [local(): normed = (widened * inv_rms * gain32).astype(jnp.bfloat16)]
    reduce_sum x1 -> x0, other arithmetic: 4.08 us -> none  [local(): jnp.mean(widened * widened, axis=1, keepdims=True) + eps]
    unnamed x23 -> x13, local copies, waits for them, and re-layouts: 10.3 us -> 7.64 us
  transfers between devices with their start and end apart: 2 -> 2, of which waited for: 0 -> 0; matrix products, arithmetic and copies ran while one was open for 24% -> 15% of each run, Pallas kernels for 61% -> 70%
where the time goes in v4:
time: 202 us; the launch traced here: 201 us
  Pallas kernels  155 us (77%)
  other arithmetic  15.7 us (8%)
  local copies, waits for them, and re-layouts  12.6 us (6%)
  matrix products  12.3 us (6%)
  starting transfers between devices  2.64 us (1%)
  between operations  2.49 us (1%)
    pallas_call x1, Pallas kernels, reduce_head(): pl.pallas_call(lambda *refs: reduce_kernel(n, *refs), name='reduce_head',...  73.6 us
    pallas_call x1, Pallas kernels, gather_window(): pl.pallas_call(lambda *refs: gather_kernel(n, *refs), name='gather_window...  66.5 us
    pallas_call x1, Pallas kernels, pooled_grads(): pl.pallas_call(lambda *refs: pool_kernel(n, *refs), name='pooled_grads',...  15.1 us
    dot_general x1, matrix products, local(): jnp.einsum('tj,td->jd', grad_logits, normed, preferred_element_type=jnp.f...  12.3 us
    unnamed x13, local copies, waits for them, and re-layouts  7.64 us
    reduce_sum x1, other arithmetic, local(): pooled = jnp.sum(weight[:, :, None] * values, axis=1) * spread  4.85 us
  transfers between devices with their start and end apart: 2, of which 0 were waited for; matrix products, arithmetic and copies ran while one was open for 15% of the time, Pallas kernels for 70%

profile of v4, /device:TPU:0, one launch (start us, length us, event | category | flops | bytes accessed | tf_op | source)
XLA Modules:
  0.0 201.1 jit_solution(1261760505211473678)
XLA Ops:
  0.6 0.7 sign_compare_fusion
  1.3 0.7 broadcast_remainder_fusion
  2.0 0.7 pad_maximum_fusion
  2.7 2.4 %collective-permute-start = (f32[8,4]{0,1:T(4,128)S(1)}, f32[8,4]{0,1:T(4,128)S(1)}, u32[]{:S(2)}, u32[]{:S(2)}) collective-permute-start(f32[8,4]{0,1:T(4,128)S(1)} %pad_maximum_fusion), channel_id=1, source_target_pairs={{8,0},{16,8},{24,16},{0,24},{9,1},{17,9},{25,17},{1,25},{10,2},{18... | collective-permute-start | bytes 392 | tf_op jit(solution)/shard_map/ppermute | solution.py:22
  5.1 0.7 bitcast_convert_fusion
  5.8 0.7 copy.35
  6.4 0.1 convert_reduce_fusion
  6.5 1.3 broadcast_in_dim.20
  7.8 0.7 compare_select_fusion.2
  8.5 0.7 convert_divide_fusion
  9.3 0.1 broadcast_bitcast_fusion
  9.3 2.2 %gather_fusion = bf16[2,128,512]{2,1,0:T(8,128)(2,1)} fusion(bf16[250,128,512]{2,1,0:T(8,128)(2,1)} %bitcast.58, s32[1024]{0:T(1024)S(1)} %pad_clamp_fusion), kind=kCustom, calls=%fused_computation | custom fusion | bytes 524296 | tf_op jit(solution)/shard_map/gather | solution.py:486
  11.6 66.5 %gather_window.1 = (bf16[1024,4096]{1,0:T(8,128)(2,1)}, f32[8,1,512]{2,1,0:T(1,128)}, bf16[768,4096]{1,0:T(8,128)(2,1)}, f32[768,1]{1,0:T(8,128)}, f32[768,1024]{1,0:T(8,128)}) custom-call(bf16[256,512]{1,0:T(8,128)(2,1)} %bitcast.52, f32[1,512]{1,0:T(1,128)} %bitcast.55, bf16[768,4096]{1,0:T(8,128)(2,1)} %bitcast.48), custom_call_target="tpu_custom_call" | custom-call | tf_op jit(solution)/shard_map/gather_window/pallas_call | solution.py:192
  78.1 0.0 copy-start.1
  78.1 4.9 %fusion.2 = f32[3,1024]{1,0:T(4,128)S(1)} fusion(f32[3,256,1024]{2,1,0:T(8,128)} %bitcast.51, f32[3,256]{1,0:T(4,128)S(1)} %convert_divide_fusion), kind=kLoop, calls=%fused_computation.6 | loop fusion | flops 6288384 | bytes 3161088 | tf_op jit(solution)/shard_map/reduce_sum | solution.py:504
  83.0 0.6 pad.8.refs_3_
  83.6 0.6 pad.7.refs_0_
  84.2 0.0 collective-permute-done
  84.2 0.0 copy-start.2
  84.2 0.7 copy.13.refs_1_
  84.9 0.0 copy-done.2
  84.9 15.1 %pooled_grads.1 = (f32[8,1024]{1,0:T(8,128)}, f32[1,128]{1,0:T(1,128)}) custom-call(f32[8,1024]{1,0:T(8,128)} %pad.7.refs_0_, f32[8,4]{1,0:T(8,128)} %copy.13.refs_1_, f32[4,8]{1,0:T(4,128)} %bitcast.56, f32[8,1024]{1,0:T(8,128)} %pad.8.refs_3_), custom_call_target="tpu_custom_call" | custom-call | tf_op jit(solution)/shard_map/pooled_grads/pallas_call | solution.py:263
  100.1 0.2 collective-permute-start.1
  100.3 0.8 slice.7
  101.1 0.0 copy-done.1
  101.1 2.5 %fusion.7.refs_1_ = bf16[768,1024]{1,0:T(8,128)(2,1)S(1)} fusion(f32[768,1024]{1,0:T(8,128)S(1)} %copy-done.1, f32[3,1024]{1,0:T(4,128)S(1)} %slice.7, f32[768]{0:T(1024)S(1)} %div.34), kind=kLoop, calls=%fused_computation.12 | loop fusion | flops 11010048 | bytes 4733952 | tf_op jit(solution)/shard_map/convert_element_type | solution.py:511
  103.6 0.0 copy-start
  103.6 12.3 %convolution_convert_fusion.refs_0_ = bf16[1024,4096]{1,0:T(8,128)(2,1)} fusion(bf16[768,1024]{1,0:T(8,128)(2,1)S(1)} %fusion.7.refs_1_, bf16[768,4096]{1,0:T(8,128)(2,1)} %get-tuple-element.17), kind=kOutput, calls=%fused_computation.3 | convolution fusion | flops 6446645248 | bytes 16252928 | tf_op jit(solution)/shard_map/tj,td->jd/dot_general | solution.py:513
  115.9 0.0 copy-done
  115.9 73.6 %reduce_head.1 = (bf16[1024,512]{1,0:T(8,128)(2,1)}, f32[1,512]{1,0:T(1,128)}, bf16[768,4096]{1,0:T(8,128)(2,1)}) custom-call(bf16[1024,4096]{1,0:T(8,128)(2,1)} %convolution_convert_fusion.refs_0_, bf16[768,1024]{1,0:T(8,128)(2,1)} %copy-done, bf16[1024,4096]{1,0:T(8,128)(2,1)} %get-tuple-element.18.refs_2_, bf16[768,4096]{1,0:T(8,128)(2,1)} %bitcast.49, ...), custom_call_target="tpu_custom_call" | custom-call | tf_op jit(solution)/shard_map/reduce_head/pallas_call | solution.py:438
  189.6 2.8 %convert_element_type.43 = f32[1024,512]{1,0:T(8,128)} convert(bf16[1024,512]{1,0:T(8,128)(2,1)} %get-tuple-element.22) | non-fusion elementwise | flops 524288 | bytes 3145728 | tf_op jit(solution)/shard_map/convert_element_type | solution.py:520
  192.4 0.0 collective-permute-done.1
  193.1 0.0 copy-start.3
  193.1 6.3 %copy.40 = bf16[1,3,256,4096]{3,2,1,0:T(8,128)(2,1)} copy(bf16[1,3,256,4096]{3,2,1,0:T(8,128)(2,1)} %bitcast.50) | data formatting | bytes 12582912
  199.3 0.0 copy-done.3
  199.3 0.6 copy.41
  (5 shorter events, 0.0 us)
Async XLA Ops:
  2.7 81.5 %collective-permute-start = (f32[8,4]{0,1:T(4,128)S(1)}, f32[8,4]{0,1:T(4,128)S(1)}, u32[]{:S(2)}, u32[]{:S(2)}) collective-permute-start(f32[8,4]{0,1:T(4,128)S(1)} %pad_maximum_fusion), channel_id=1, source_target_pairs={{8,0},{16,8},{24,16},{0,24},{9,1},{17,9},{25,17},{1,25},{10,2},{18... | collective-permute-start | bytes 392 | tf_op jit(solution)/shard_map/ppermute | solution.py:22
  78.1 23.0 %copy-start.1 = (f32[768,1024]{1,0:T(8,128)S(1)}, f32[768,1024]{1,0:T(8,128)}, u32[]{:S(2)}) copy-start(f32[768,1024]{1,0:T(8,128)} %get-tuple-element.14) | copy-start | bytes 9437188
  84.2 0.7 copy-start.2
  100.1 92.3 %collective-permute-start.1 = (f32[1]{0:T(128)}, f32[1]{0:T(128)}, u32[]{:S(2)}, u32[]{:S(2)}) collective-permute-start(f32[1]{0:T(128)} %bitcast.62), channel_id=1, source_target_pairs={{24,0},{0,8},{8,16},{16,24},{25,1},{1,9},{9,17},{17,25},{26,2},{2,... | collective-permute-start | bytes 20 | tf_op jit(solution)/shard_map/ppermute | solution.py:22
  103.6 12.3 %copy-start = (bf16[768,1024]{1,0:T(8,128)(2,1)}, bf16[768,1024]{1,0:T(8,128)(2,1)S(1)}, u32[]{:S(2)}) copy-start(bf16[768,1024]{1,0:T(8,128)(2,1)S(1)} %fusion.7.refs_1_) | copy-start | bytes 4718596
  193.1 6.3 %copy-start.3 = (f32[1,512]{1,0:T(1,128)S(1)}, f32[1,512]{1,0:T(1,128)}, u32[]{:S(2)}) copy-start(f32[1,512]{1,0:T(1,128)} %get-tuple-element.23) | copy-start | bytes 6148
